TPU v7x, 128 devices: a whole 4x4x4 slice. The times are simulated.
128 devices in a mesh: rg: 4 (over y_hi, core), az: 32 (over y_lo, x, z).
Axes of the slice: x: 4, y: 4 (y_hi: 2, y_lo: 2; y = y_hi * 2 + y_lo), z: 4, core: 2. Of those that a mesh axis runs over, the one named last changes fastest.
Arguments:
- raw_pulses: bfloat16 [2, 2048, 65536], P(None, ('rg', 'az')), may hold values from -6 to 6
- range_phase: float32 [65536], replicated, may hold values from -3.140625 to 3.140625
- azimuth_rate: float32 [65536], P(('rg', 'az')), may hold values from 40 to 400
- conc_azimuth: float32 [2048], replicated, may hold values from 0.2 to 1
- conc_range: float32 [65536], replicated, may hold values from 0.2 to 1
Outputs:
- edge_azimuth: float32 [2048, 65536], P(None, ('rg', 'az'))
- edge_range: float32 [2048, 65536], P(('rg', 'az'))
All inputs are finite; a program needn't handle non-finite values.
Results may differ from a plain program's by a relative error of at most 0.028.
Values may be sent and summed in bfloat16 or wider, within the bound.
No kernel may reach another device: no remote copies, remote signals or barrier semaphores. Data moves between devices by JAX's collectives and lax.ppermute only.
A program may use at most 128 MiB of HBM per device.

v0:
```python
import math

import jax
import jax.numpy as jnp
import numpy as np
from jax import lax
from jax.experimental import pallas as pl
from jax.experimental.pallas import tpu as pltpu
from jax.sharding import PartitionSpec as P

AXES = ("rg", "az")
BINS = 65536
PULSES = 2048
ROWS = 16
OWNERS = 128
WIDTH = 512
LOW = jnp.bfloat16
F32 = jnp.float32


def roots(exponents, length):
    angles = 2.0 * math.pi / length * (exponents % length)
    return np.cos(angles) + 1j * np.sin(angles)


def left_form(matrix):
    return np.block([[matrix.real, -matrix.imag], [matrix.imag, matrix.real]])


def right_form(matrix):
    return np.block([[matrix.real, matrix.imag], [-matrix.imag, matrix.real]])


def low(table):
    return np.asarray(table, np.float32).astype(LOW)


def range_tables():
    k = np.arange(128)[:, None]
    j = np.arange(128)[None, :]
    even = roots(2 * j * k, 256) / 16.0
    odd = roots((2 * j + 1) * k, 256) / 16.0
    first = np.stack([left_form(even.conj()), left_form(odd.conj())])
    second = np.stack([right_form(even.conj()), right_form(odd.conj())])
    third = np.stack([right_form(even.T), right_form(odd.T)])
    fourth = np.stack([left_form(even.T), left_form(odd.T)])
    return tuple(low(t) for t in (first, second, third, fourth))


def range_turns(rows):
    table = roots(np.arange(rows)[:, None] * np.arange(256)[None, :], BINS)
    return np.stack([table.real, table.imag]).astype(np.float32)


def real_range_tables():
    k = np.arange(128)[:, None]
    n = np.concatenate([2 * np.arange(128), 2 * np.arange(128) + 1])[None, :]
    base = roots(k * n, 256) / 16.0
    mirror = np.cos(math.pi * n) / 16.0
    first = np.concatenate([base.real, mirror, -base.imag[1:]], 0)
    last = np.concatenate([base.real.T, mirror.T, -base.imag[1:].T], 1)
    return low(first), low(last)


def azimuth_tables():
    s = np.arange(128)
    outer = roots(-s[:, None] * s[None, :], 128) / math.sqrt(128.0)
    full = left_form(outer).reshape(2, 16, 8, 256).transpose(1, 0, 2, 3).reshape(256, 256)
    group = np.arange(16)[:, None, None, None]
    eight = np.arange(8)[None, None, None, :]
    fb = np.arange(16)[None, :, None, None]
    p = np.arange(16)[None, None, :, None]
    inner = roots(-p * (8 * group + eight + 128 * fb), PULSES) / 4.0
    pair = np.stack([np.stack([inner.real, -inner.imag], 3), np.stack([inner.imag, inner.real], 3)], 2)
    forward = pair.reshape(16, 32, 256)
    backward = pair.transpose(0, 3, 4, 1, 2, 5).reshape(16, 32, 256)
    return low(full), low(full.T), low(forward), low(backward)


def dot(a, b):
    return jnp.dot(a, b, preferred_element_type=F32)


def beside(a, b):
    return jnp.concatenate([a, b], 1)


def above(a, b):
    return jnp.concatenate([a, b], 0)


def forward_spectrum(parts, turns, second):
    sums, gaps = [], []
    for re, im, rows in parts:
        c, s = turns[0, rows, :], turns[1, rows, :]
        tr = re * c + im * s
        ti = im * c - re * s
        sums.append(beside(tr[:, :128] + tr[:, 128:], ti[:, :128] + ti[:, 128:]).astype(LOW))
        gaps.append(beside(tr[:, :128] - tr[:, 128:], ti[:, :128] - ti[:, 128:]).astype(LOW))
    return (
        dot(jnp.concatenate(sums, 0), second[0]),
        dot(jnp.concatenate(gaps, 0), second[1]),
    )


def back_section(even, odd, turns, third):
    even = dot(even, third[0])
    odd = dot(odd, third[1])
    rows = even.shape[0]
    halves = []
    for h, b in enumerate((even + odd, even - odd)):
        c = turns[0, :rows, h * 128 : h * 128 + 128]
        s = turns[1, :rows, h * 128 : h * 128 + 128]
        re, im = b[:, :128], b[:, 128:]
        halves.append((re * c - im * s, re * s + im * c))
    return halves


def compress_kernel(raw, phase, first, second, third, fourth, turns, out, xs, os):
    def spread(n, _):
        for u in range(4):
            at = n * 4 + u
            for c in range(2):
                v = raw[c, :, pl.ds(pl.multiple_of(at * 256, 256), 256)].astype(F32)
                row = pl.multiple_of(at * ROWS, ROWS)
                xs[c, 0, pl.ds(row, ROWS), :] = v[:, :128]
                xs[c, 1, pl.ds(row, ROWS), :] = v[:, 128:]
        return 0

    lax.fori_loop(0, 64, spread, 0)

    def one(p):
        def load(odd):
            def half(c):
                at = pl.ds(odd * ROWS + p, 128, stride=2 * ROWS)
                return beside(xs[c, 0, at, :], xs[c, 1, at, :])

            return above(half(0), half(1)).astype(LOW)

        even = dot(first[0], load(0))
        odd = dot(first[1], load(1))
        lo, hi = even + odd, even - odd
        parts = [(v[:128], v[128:], slice(r, r + 128)) for v, r in ((lo, 0), (hi, 128))]
        turned = []
        for e, z in enumerate(forward_spectrum(parts, turns, second)):
            c = phase[0, :, e * 128 : e * 128 + 128]
            s = phase[1, :, e * 128 : e * 128 + 128]
            re, im = z[:, :128], z[:, 128:]
            turned.append(beside(re * c - im * s, re * s + im * c).astype(LOW))
        (r0, i0), (r1, i1) = back_section(turned[0], turned[1], turns, third)
        re, im = beside(r0, r1), beside(i0, i1)
        sums = above(re[:128] + re[128:], im[:128] + im[128:]).astype(LOW)
        gaps = above(re[:128] - re[128:], im[:128] - im[128:]).astype(LOW)
        for o, c in enumerate((dot(fourth[0], sums), dot(fourth[1], gaps))):
            for part in range(2):
                for h in range(2):
                    os[part * 4 + o * 2 + h, pl.ds(p, 128, stride=ROWS), :] = c[
                        part * 128 : part * 128 + 128, h * 128 : h * 128 + 128
                    ]

    def pair(i, _):
        one(2 * i)
        one(2 * i + 1)
        return 0

    lax.fori_loop(0, ROWS // 2, pair, 0)

    def gather(n, _):
        rows = pl.ds(pl.multiple_of(n * 128, 128), 128)
        for k in range(8):
            v = os[k, rows, :].astype(LOW).reshape(8, ROWS, 128)
            out[pl.ds(n * 8, 8), :, k * 128 : k * 128 + 128] = v
        return 0

    lax.fori_loop(0, 16, gather, 0)


def range_compress(raw, phase, tables, turns):
    return pl.pallas_call(
        compress_kernel,
        out_shape=jax.ShapeDtypeStruct((OWNERS, ROWS, 1024), LOW),
        scratch_shapes=[
            pltpu.VMEM((2, 2, 256 * ROWS, 128), F32),
            pltpu.VMEM((8, OWNERS * ROWS, 128), F32),
        ],
        name="range_compress",
    )(raw, phase, *tables, turns)


def spread_rows(source, xs):
    def move(n, _):
        rows = pl.ds(pl.multiple_of(n * 128, 128), 128)
        for h in range(2):
            v = source[pl.ds(n * 8, 8), :, h * 128 : h * 128 + 128].astype(F32)
            xs[h, rows, :] = v.reshape(128, 128)
        return 0

    lax.fori_loop(0, 16, move, 0)


def pulse_rows(xs, p):
    at = pl.ds(p, 128, stride=ROWS)
    return beside(xs[0, at, :], xs[1, at, :])


def picture_kernel(re, im, phase, full, back, forward, backward, out, xr, xi, ys, vs, ms):
    spread_rows(re, xr)
    spread_rows(im, xi)

    def outer(p, _):
        x = above(pulse_rows(xr, p), pulse_rows(xi, p)).astype(LOW)
        ys[p] = dot(full[...], x).astype(LOW)
        return 0

    lax.fori_loop(0, 16, outer, 0, unroll=4)

    def inner(g, _):
        rows = pl.ds(pl.multiple_of(g * 16, 16), 16)
        y = dot(forward[g], ys[:, rows, :].reshape(256, 256)).reshape(16, 2, 8, 256)
        c = phase[0, g].reshape(16, 8, 256)
        s = phase[1, g].reshape(16, 8, 256)
        zr = y[:, 0] * c - y[:, 1] * s
        zi = y[:, 0] * s + y[:, 1] * c
        z = jnp.stack([zr, zi], 1).reshape(256, 256).astype(LOW)
        vs[:, rows, :] = dot(backward[g], z).astype(LOW).reshape(16, 16, 256)
        return 0

    lax.fori_loop(0, 16, inner, 0, unroll=2)

    def last(p, _):
        x = dot(back[...], vs[p])
        a, b = x[:128], x[128:]
        m = jnp.sqrt(a * a + b * b)
        at = pl.ds(p, 128, stride=ROWS)
        ms[0, at, :] = m[:, :128]
        ms[1, at, :] = m[:, 128:]
        return 0

    lax.fori_loop(0, 16, last, 0, unroll=4)

    def gather(n, _):
        rows = pl.ds(pl.multiple_of(n * 128, 128), 128)
        for h in range(2):
            v = ms[h, rows, :].astype(LOW).reshape(8, ROWS, 128)
            out[pl.ds(n * 8, 8), :, h * 128 : h * 128 + 128] = v
        return 0

    lax.fori_loop(0, 16, gather, 0)


def whole(shape):
    return pl.BlockSpec(shape, lambda i: (0,) * len(shape))


def azimuth_picture(received, phase, full, back, forward, backward):
    return pl.pallas_call(
        picture_kernel,
        grid=(2,),
        in_specs=[
            pl.BlockSpec((OWNERS, ROWS, 256), lambda i: (0, 0, i)),
            pl.BlockSpec((OWNERS, ROWS, 256), lambda i: (0, 0, i + 2)),
            pl.BlockSpec((2, 16, 128, 256), lambda i: (0, 0, 0, i)),
            whole((256, 256)),
            whole((256, 256)),
            whole((16, 256, 256)),
            whole((16, 256, 256)),
        ],
        out_specs=pl.BlockSpec((OWNERS, ROWS, 256), lambda i: (0, 0, i)),
        out_shape=jax.ShapeDtypeStruct((OWNERS, ROWS, WIDTH), LOW),
        scratch_shapes=[
            pltpu.VMEM((2, PULSES, 128), F32),
            pltpu.VMEM((2, PULSES, 128), F32),
            pltpu.VMEM((16, 256, 256), LOW),
            pltpu.VMEM((16, 256, 256), LOW),
            pltpu.VMEM((2, PULSES, 128), F32),
        ],
        name="azimuth_picture",
    )(received, received, phase, full, back, forward, backward)


def edge_kernel(mag, weights, full, back, forward, backward, out, xs, ys, vs, ms):
    spread_rows(mag, xs)

    def outer(p, _):
        ys[p] = dot(full[:, :128], pulse_rows(xs, p).astype(LOW)).astype(LOW)
        return 0

    lax.fori_loop(0, 16, outer, 0, unroll=4)

    def inner(g, _):
        rows = pl.ds(pl.multiple_of(g * 16, 16), 16)
        y = dot(forward[g], ys[:, rows, :].reshape(256, 256)).reshape(16, 2, 8, 256)
        w = weights[g]
        w = beside(w, w).reshape(16, 8, 256)
        z = jnp.stack([-y[:, 1] * w, y[:, 0] * w], 1).reshape(256, 256).astype(LOW)
        vs[:, rows, :] = dot(backward[g], z).astype(LOW).reshape(16, 16, 256)
        return 0

    lax.fori_loop(0, 16, inner, 0, unroll=2)

    def last(p, _):
        x = dot(back[:128, :], vs[p])
        at = pl.ds(p, 128, stride=ROWS)
        ms[0, at, :] = x[:, :128]
        ms[1, at, :] = x[:, 128:]
        return 0

    lax.fori_loop(0, 16, last, 0, unroll=4)

    def gather(n, _):
        rows = pl.ds(pl.multiple_of(n * 128, 128), 128)
        out[rows, :128] = ms[0, rows, :]
        out[rows, 128:] = ms[1, rows, :]
        return 0

    lax.fori_loop(0, 16, gather, 0)


def azimuth_edges(mag, weights, full, back, forward, backward):
    return pl.pallas_call(
        edge_kernel,
        grid=(2,),
        in_specs=[
            pl.BlockSpec((OWNERS, ROWS, 256), lambda i: (0, 0, i)),
            whole((16, 128, 128)),
            whole((256, 256)),
            whole((256, 256)),
            whole((16, 256, 256)),
            whole((16, 256, 256)),
        ],
        out_specs=pl.BlockSpec((PULSES, 256), lambda i: (0, i)),
        out_shape=jax.ShapeDtypeStruct((PULSES, WIDTH), F32),
        scratch_shapes=[
            pltpu.VMEM((2, PULSES, 128), F32),
            pltpu.VMEM((16, 256, 256), LOW),
            pltpu.VMEM((16, 256, 256), LOW),
            pltpu.VMEM((2, PULSES, 128), F32),
        ],
        name="azimuth_edges",
    )(mag, weights, full, back, forward, backward)


def concentrate_kernel(mag, weights, first, second, third, last, turns, out, xs, os):
    def spread(n, _):
        rows = pl.ds(pl.multiple_of(n * 128, 128), 128)
        for k in range(4):
            v = mag[pl.ds(n * 8, 8), :, k * 128 : k * 128 + 128].astype(F32)
            xs[k, rows, :] = v.reshape(128, 128)
        return 0

    lax.fori_loop(0, 16, spread, 0)
    top = lax.broadcasted_iota(jnp.int32, (128, 256), 0) == 0

    def one(p):
        at = pl.ds(p, 128, stride=ROWS)
        x = above(beside(xs[0, at, :], xs[1, at, :]), beside(xs[2, at, :], xs[3, at, :]))
        y = dot(first[...], x.astype(LOW))
        re, im = y[:128], y[128:]
        mirror = jnp.where(top[:16], im[:16], 0.0)
        im = jnp.where(top, 0.0, im)
        parts = [(re, im, slice(0, 128)), (mirror, jnp.zeros_like(mirror), slice(128, 144))]
        jumped = []
        for e, z in enumerate(forward_spectrum(parts, turns, second)):
            w = weights[:, e * 128 : e * 128 + 128]
            jumped.append(beside(-z[:, 128:] * w, z[:, :128] * w).astype(LOW))
        (r0, i0), (r1, i1) = back_section(jumped[0], jumped[1], turns, third)
        re, im = beside(r0, r1), beside(i0, i1)
        im = above(jnp.where(top[:8], re[128:136], im[:8]), im[8:128])
        e = dot(last[...], above(re[:128], im).astype(LOW))
        for o in range(2):
            for h in range(2):
                os[h, pl.ds(o * ROWS + p, 128, stride=2 * ROWS), :] = e[
                    o * 128 : o * 128 + 128, h * 128 : h * 128 + 128
                ]

    def pair(i, _):
        one(2 * i)
        one(2 * i + 1)
        return 0

    lax.fori_loop(0, ROWS // 2, pair, 0)

    def gather(n, _):
        for u in range(4):
            at = n * 4 + u
            rows = pl.ds(pl.multiple_of(at * ROWS, ROWS), ROWS)
            out[:, pl.ds(pl.multiple_of(at * 256, 256), 256)] = beside(os[0, rows, :], os[1, rows, :])
        return 0

    lax.fori_loop(0, 64, gather, 0)


def range_concentrate(mag, weights, first, second, third, last, turns):
    return pl.pallas_call(
        concentrate_kernel,
        out_shape=jax.ShapeDtypeStruct((ROWS, BINS), F32),
        scratch_shapes=[
            pltpu.VMEM((4, PULSES, 128), F32),
            pltpu.VMEM((2, 256 * ROWS, 128), F32),
        ],
        name="range_concentrate",
    )(mag, weights, first, second, third, last, turns)


def signed(freqs, length):
    return jnp.where(freqs < length // 2, freqs, freqs - length)


def split_grid(values):
    grid = values.reshape(128, 2, 256)
    return grid.transpose(2, 1, 0).reshape(256, 256)


def azimuth_phase(rates):
    freqs = jnp.arange(PULSES, dtype=jnp.int32).reshape(16, 16, 8).transpose(1, 0, 2)
    s = signed(freqs, PULSES).astype(F32).reshape(16, 128, 1) / PULSES
    angles = (s * s) * rates[None, None, :]
    return jnp.stack([jnp.cos(angles), jnp.sin(angles)])


def azimuth_weights(factors):
    freqs = jnp.arange(PULSES, dtype=jnp.int32)
    values = jnp.sign(signed(freqs, PULSES)).astype(F32) * factors
    values = values.reshape(16, 16, 8).transpose(1, 0, 2).reshape(16, 128, 1)
    return jnp.broadcast_to(values, (16, 128, 128))


def range_weights(factors):
    freqs = jnp.arange(BINS, dtype=jnp.int32)
    signs = jnp.sign(signed(freqs, BINS)).astype(F32)
    partner = jnp.roll(jnp.flip(factors), 1)
    inside = freqs % 128 != 0
    values = signs * jnp.where(inside, factors + partner, factors)
    return split_grid(values)[:144]


def expand(compact):
    row = lax.broadcasted_iota(jnp.int32, (1, 1, 8, 256), 2)
    lane = lax.broadcasted_iota(jnp.int32, (1, 1, 8, 256), 3)
    kept = jnp.where(lane % 8 == row, compact[:, :, None, :], jnp.zeros((), LOW))
    return kept.reshape(16, 256, 256)


def on_device(raw_pulses, range_phase, azimuth_rate, conc_azimuth, conc_range):
    first, second, third, fourth = range_tables()
    turns = jnp.asarray(range_turns(256))
    grid = split_grid(range_phase)
    phase = jnp.stack([jnp.cos(grid), jnp.sin(grid)])
    blocks = range_compress(raw_pulses, phase, (first, second, third, fourth), turns)
    received = lax.all_to_all(blocks, AXES, split_axis=0, concat_axis=0, tiled=True)
    full, back, forward, backward = azimuth_tables()
    forward, backward, _ = lax.optimization_barrier((forward, backward, conc_azimuth))
    forward, backward = expand(forward), expand(backward)
    turn = azimuth_phase(azimuth_rate)
    mag = azimuth_picture(received, turn, full, back, forward, backward)
    shared = lax.all_to_all(mag, AXES, split_axis=0, concat_axis=0, tiled=True)
    edge_azimuth = azimuth_edges(mag, azimuth_weights(conc_azimuth), full, back, forward, backward)
    real_first, real_last = real_range_tables()
    edge_range = range_concentrate(
        shared, range_weights(conc_range), real_first, second, third, real_last, turns
    )
    return (edge_azimuth, edge_range)


def solution(mesh):
    in_specs = (P(None, AXES, None), P(), P(AXES), P(), P())
    out_specs = (P(None, AXES), P(AXES, None))
    return jax.shard_map(
        on_device, mesh=mesh, in_specs=in_specs, out_specs=out_specs, check_vma=False
    )
```

profile of v0, /device:TPU:0, one launch (start us, length us, event | category | flops | bytes accessed | tf_op | source)
XLA Modules:
  0.0 168.6 jit_solution(3932001088551605809)
XLA Ops:
  0.6 1.9 %fusion.14 = (f32[65536]{0:T(1024)S(1)}, f32[65536]{0:T(1024)S(1)}) fusion(f32[65536]{0:T(1024)} %param.17), kind=kLoop, calls=%fused_computation.32 | loop fusion | bytes 786432 | tf_op jit(solution)/shard_map/cos | solution.py:448
  2.5 0.2 sin.30
  2.7 0.2 copy.19
  2.8 0.2 sin.32
  3.1 0.2 cos.30
  3.2 0.2 copy.18
  3.4 0.2 cos.32
  3.6 0.8 pad_maximum_fusion.1.phase
  4.4 24.7 %range_compress.1 = bf16[128,16,1024]{2,1,0:T(8,128)(2,1)} custom-call(bf16[2,16,65536]{2,1,0:T(8,128)(2,1)} %raw.1, f32[2,256,256]{2,1,0:T(8,128)} %pad_maximum_fusion.1.phase, bf16[2,256,256]{2,1,0:T(8,128)(2,1)} %constant.78.clone.first, bf16[2,256,256]{2,1,0:T(8,128)(2,1)} %constant.79.clone.second, bf16[2,256,256]{2,1,0:T(8,128)(2,1)} %constant.80.clone.third, ...), custom_call_target="tpu_custom_call" | custom-call | tf_op jit(solution)/shard_map/range_compress/pallas_call | solution.py:179
  29.1 0.0 copy-start.5
  29.1 11.9 %all-to-all-start = ((bf16[128,16,1024]{2,1,0:T(8,128)(2,1)}), bf16[128,16,1024]{2,1,0:T(8,128)(2,1)}, u32[]{:S(2)}, u32[]{:S(2)}) async-start(bf16[128,16,1024]{2,1,0:T(8,128)(2,1)} %range_compress.1), calls=%async_computation | async-start | bytes 8388608 | tf_op jit(solution)/shard_map/all_to_all | solution.py:450
  41.0 0.1 reshape.181
  41.1 0.1 iota.64
  41.3 0.0 copy-done.5
  41.3 14.7 %multiply_cosine_fusion = (f32[1,16,128,512]{3,2,1,0:T(8,128)S(1)}, f32[1,16,128,512]{3,2,1,0:T(8,128)S(1)}) fusion(f32[512]{0:T(512)S(1)} %copy-done.5, f32[16,128]{1,0:T(8,128)S(1)} %fusion.9), kind=kLoop, calls=%fused_computation.2 | loop fusion | flops 1048576 | bytes 8398848 | tf_op jit(solution)/shard_map/cos | solution.py:418
  56.0 0.0 copy-start.2
  56.0 0.0 copy-start.3
  56.0 4.2 %pad_maximum_fusion.phase = f32[2,16,128,512]{3,2,1,0:T(8,128)} fusion(f32[1,16,128,512]{3,2,1,0:T(8,128)S(1)} %get-tuple-element.11, f32[1,16,128,512]{3,2,1,0:T(8,128)S(1)} %get-tuple-element.10), kind=kLoop, calls=%fused_computation | loop fusion | flops 2097152 | bytes 16777216 | tf_op jit(solution)/shard_map/stack | solution.py:418
  60.3 0.0 copy-done.2
  60.3 0.0 copy-done.3
  60.3 2.5 %bitcast_select_fusion = (bf16[16,256,256]{2,1,0:T(8,128)(2,1)}, bf16[16,256,256]{2,1,0:T(8,128)(2,1)}) fusion(pred[256,256]{1,0:T(8,128)(4,1)S(1)} %broadcast_bitcast_fusion, bf16[16,32,256]{2,1,0:T(8,128)(2,1)S(1)} %copy-done.3, bf16[16,32,256]{2,1,0:T(8,128)(2,1)S(1)} %copy-done.2), kind=kLoop, calls=%fused_computation.3 | loop fusion | flops 2097152 | bytes 4784128 | tf_op jit(solution)/shard_map/jit(_where)/select_n | solution.py:440
  62.8 29.5 %all-to-all-done.re.im = bf16[128,16,1024]{2,1,0:T(8,128)(2,1)} async-done(((bf16[128,16,1024]{2,1,0:T(8,128)(2,1)}), bf16[128,16,1024]{2,1,0:T(8,128)(2,1)}, u32[]{:S(2)}, u32[]{:S(2)}) %all-to-all-start) | async-done | bytes 4194336 | tf_op jit(solution)/shard_map/all_to_all | solution.py:450
  92.3 21.8 %azimuth_picture.1.mag = bf16[128,16,512]{2,1,0:T(8,128)(2,1)} custom-call(bf16[128,16,1024]{2,1,0:T(8,128)(2,1)} %all-to-all-done.re.im, bf16[128,16,1024]{2,1,0:T(8,128)(2,1)} %all-to-all-done.re.im, f32[2,16,128,512]{3,2,1,0:T(8,128)} %pad_maximum_fusion.phase, bf16[256,256]{1,0:T(8,128)(2,1)} %constant.84.clone.full, ...), custom_call_target="tpu_custom_call" | custom-call | tf_op jit(solution)/shard_map/azimuth_picture/pallas_call | solution.py:256
  114.1 0.0 copy-start.1
  114.1 0.0 copy-start.4
  114.1 5.9 %all-to-all-start.1 = ((bf16[128,16,512]{2,1,0:T(8,128)(2,1)}), bf16[128,16,512]{2,1,0:T(8,128)(2,1)S(1)}, u32[]{:S(2)}, u32[]{:S(2)}) async-start(bf16[128,16,512]{2,1,0:T(8,128)(2,1)} %azimuth_picture.1.mag), calls=%async_computation.1 | async-start | bytes 4194304 | tf_op jit(solution)/shard_map/all_to_all | solution.py:456
  120.0 0.0 copy-done.1
  120.0 0.1 slice.19
  120.1 0.5 slice.18
  120.6 0.0 copy-done.4
  120.7 0.1 reshape.183
  120.8 0.1 copy.20
  120.8 0.1 copy.21
  120.9 0.4 reverse.2
  121.3 0.1 slice.24
  121.4 0.8 fusion.1
  122.2 0.2 reshape.184
  122.4 0.2 copy.22
  122.6 0.7 copy.25
  123.2 1.3 broadcast_in_dim.62.weights
  124.5 18.1 %azimuth_edges.1 = f32[2048,512]{1,0:T(8,128)} custom-call(bf16[128,16,512]{2,1,0:T(8,128)(2,1)} %azimuth_picture.1.mag, f32[16,128,128]{2,1,0:T(8,128)} %broadcast_in_dim.62.weights, bf16[256,256]{1,0:T(8,128)(2,1)} %constant.84.clone.full, bf16[256,256]{1,0:T(8,128)(2,1)} %constant.85.clone.back, bf16[16,256,256]{2,1,0:T(8,128)(2,1)} %get-tuple-element.9.forward, ...), custom_call_target="tpu_custom_call" | custom-call | tf_op jit(solution)/shard_map/azimuth_edges/pallas_call | solution.py:320
  142.6 6.9 %all-to-all-done.1.mag = bf16[128,16,512]{2,1,0:T(8,128)(2,1)S(1)} async-done(((bf16[128,16,512]{2,1,0:T(8,128)(2,1)}), bf16[128,16,512]{2,1,0:T(8,128)(2,1)S(1)}, u32[]{:S(2)}, u32[]{:S(2)}) %all-to-all-start.1) | async-done | bytes 2097184 | tf_op jit(solution)/shard_map/all_to_all | solution.py:456
  149.5 0.0 copy-start
  149.5 1.3 copy-done
  150.9 17.7 %range_concentrate.1 = f32[16,65536]{1,0:T(8,128)} custom-call(bf16[128,16,512]{2,1,0:T(8,128)(2,1)} %copy-done, f32[144,256]{1,0:T(8,128)} %bitcast.22, bf16[256,256]{1,0:T(8,128)(2,1)} %constant.86.clone.first, bf16[2,256,256]{2,1,0:T(8,128)(2,1)} %constant.79.clone.second, bf16[2,256,256]{2,1,0:T(8,128)(2,1)} %constant.80.clone.third, ...), custom_call_target="tpu_custom_call" | custom-call | tf_op jit(solution)/shard_map/range_concentrate/pallas_call | solution.py:394
  (8 shorter events, 0.1 us)
Async XLA Ops:
  29.1 12.2 %copy-start.5 = (f32[512]{0:T(512)S(1)}, f32[512]{0:T(512)}, u32[]{:S(2)}) copy-start(f32[512]{0:T(512)} %param.18) | copy-start | bytes 6148
  29.1 63.1 %all-to-all-start = ((bf16[128,16,1024]{2,1,0:T(8,128)(2,1)}), bf16[128,16,1024]{2,1,0:T(8,128)(2,1)}, u32[]{:S(2)}, u32[]{:S(2)}) async-start(bf16[128,16,1024]{2,1,0:T(8,128)(2,1)} %range_compress.1), calls=%async_computation | async-start | bytes 8388608 | tf_op jit(solution)/shard_map/all_to_all | solution.py:450
  56.0 4.3 %copy-start.2 = (bf16[16,32,256]{2,1,0:T(8,128)(2,1)S(1)}, bf16[16,32,256]{2,1,0:T(8,128)(2,1)}, u32[]{:S(2)}) copy-start(bf16[16,32,256]{2,1,0:T(8,128)(2,1)} %constant.82.clone) | copy-start | bytes 786436
  56.0 4.3 %copy-start.3 = (bf16[16,32,256]{2,1,0:T(8,128)(2,1)S(1)}, bf16[16,32,256]{2,1,0:T(8,128)(2,1)}, u32[]{:S(2)}) copy-start(bf16[16,32,256]{2,1,0:T(8,128)(2,1)} %constant.83.clone) | copy-start | bytes 786436
  114.1 5.9 %copy-start.1 = (f32[65536]{0:T(1024)S(1)}, f32[65536]{0:T(1024)}, u32[]{:S(2)}) copy-start(f32[65536]{0:T(1024)} %param.20) | copy-start | bytes 786436
  114.1 6.6 %copy-start.4 = (f32[2048]{0:T(1024)S(1)}, f32[2048]{0:T(1024)}, u32[]{:S(2)}) copy-start(f32[2048]{0:T(1024)} %param.19) | copy-start | bytes 24580
  114.1 35.5 %all-to-all-start.1 = ((bf16[128,16,512]{2,1,0:T(8,128)(2,1)}), bf16[128,16,512]{2,1,0:T(8,128)(2,1)S(1)}, u32[]{:S(2)}, u32[]{:S(2)}) async-start(bf16[128,16,512]{2,1,0:T(8,128)(2,1)} %azimuth_picture.1.mag), calls=%async_computation.1 | async-start | bytes 4194304 | tf_op jit(solution)/shard_map/all_to_all | solution.py:456
  149.5 1.3 copy-start
where the time goes:
time: 169 us
  Pallas kernels  82.3 us (49%)
  waiting for transfers between devices  36.4 us (22%)
  other arithmetic  23.1 us (14%)
  starting transfers between devices  17.8 us (11%)
  local copies, waits for them, and re-layouts  8.16 us (5%)
    all_to_all x1, waiting for transfers between devices, on_device(): lax.all_to_all(blocks, AXES, split_axis=0, concat_axis=0, tiled=True)  29.5 us
    pallas_call x1, Pallas kernels, range_compress(): pl.pallas_call(compress_kernel, out_shape=jax.ShapeDtypeStruct((OWNERS, R...  24.7 us
    pallas_call x1, Pallas kernels, azimuth_picture(): pl.pallas_call(picture_kernel, grid=(2,), in_specs=[pl.BlockSpec((OWNERS,...  21.8 us
    pallas_call x1, Pallas kernels, azimuth_edges(): pl.pallas_call(edge_kernel, grid=(2,), in_specs=[pl.BlockSpec((OWNERS, RO...  18.1 us
    pallas_call x1, Pallas kernels, range_concentrate(): pl.pallas_call(concentrate_kernel, out_shape=jax.ShapeDtypeStruct((ROWS,...  17.7 us
    cos x1, other arithmetic, azimuth_phase(): return jnp.stack([jnp.cos(angles), jnp.sin(angles)])  14.7 us
    all_to_all x1, starting transfers between devices, on_device(): lax.all_to_all(blocks, AXES, split_axis=0, concat_axis=0, tiled=True)  11.9 us
    all_to_all x1, waiting for transfers between devices, on_device(): shared = lax.all_to_all(mag, AXES, split_axis=0, concat_axis=0, tiled=True)  6.92 us
  transfers between devices with their start and end apart: 2, of which 2 were waited for; matrix products, arithmetic and copies ran while one was open for 16% of the time, Pallas kernels for 11%

commit v1 on v0

--- a/solution.py
+++ b/solution.py
@@ -12,6 +12,8 @@
 BINS = 65536
 PULSES = 2048
 ROWS = 16
+PITCH = 18
+FILLS = 4
 OWNERS = 128
 WIDTH = 512
 LOW = jnp.bfloat16
@@ -89,6 +91,15 @@
     return jnp.concatenate([a, b], 0)
 
 
+def whole(shape):
+    return pl.BlockSpec(shape, lambda i: (0,) * len(shape), pipeline_mode=pl.Buffered(1))
+
+
+def together(jobs):
+    while jobs:
+        jobs = [job for job in jobs if next(job, None) is not None]
+
+
 def forward_spectrum(parts, turns, second):
     sums, gaps = [], []
     for re, im, rows in parts:
@@ -116,29 +127,73 @@
     return halves
 
 
-def compress_kernel(raw, phase, first, second, third, fourth, turns, out, xs, os):
-    def spread(n, _):
-        for u in range(4):
-            at = n * 4 + u
-            for c in range(2):
-                v = raw[c, :, pl.ds(pl.multiple_of(at * 256, 256), 256)].astype(F32)
-                row = pl.multiple_of(at * ROWS, ROWS)
-                xs[c, 0, pl.ds(row, ROWS), :] = v[:, :128]
-                xs[c, 1, pl.ds(row, ROWS), :] = v[:, 128:]
-        return 0
-
-    lax.fori_loop(0, 64, spread, 0)
-
+def sine_cosine(x):
+    t = 0.5 * x
+    u = t * t
+    s = 1.0 / 39916800.0
+    for k in (362880.0, -5040.0, 120.0, -6.0, 1.0):
+        s = 1.0 / k + u * s if k != 362880.0 else 1.0 / k - u * s
+    s = s * t
+    c = 1.0 / 479001600.0
+    for k in (-3628800.0, 40320.0, -720.0, 24.0, -2.0, 1.0):
+        c = 1.0 / k + u * c
+    return 2.0 * s * c, 1.0 - 2.0 * s * s
+
+
+def compress_kernel(raw, angles, first, second, third, fourth, turns, out, xs, os, phase):
+    step = pl.program_id(0)
+
+    @pl.when(step == 0)
+    def _():
+        sine, cosine = sine_cosine(angles[...].T)
+        for e in range(2):
+            phase[0, :, e * 128 : e * 128 + 128] = cosine[e * 256 : e * 256 + 256]
+            phase[1, :, e * 128 : e * 128 + 128] = sine[e * 256 : e * 256 + 256]
+
+    @pl.when(step < FILLS)
+    def _():
+        def spread(n, _):
+            for u in range(4):
+                at = n * 4 + u
+                for c in range(2):
+                    v = raw[c, :, pl.ds(pl.multiple_of(at * 256, 256), 256)].astype(F32)
+                    row = (step * (256 // FILLS) + at) * PITCH
+                    xs[c, 0, pl.ds(row, ROWS), :] = v[:, :128]
+                    xs[c, 1, pl.ds(row, ROWS), :] = v[:, 128:]
+            return 0
+
+        lax.fori_loop(0, 64 // FILLS, spread, 0)
+
+    @pl.when(step == FILLS - 1)
+    def _():
+        compress_pulses(first, second, third, fourth, turns, xs, os, phase)
+
+    @pl.when(step >= FILLS)
+    def _():
+        def gather(n, _):
+            for u in range(4):
+                at = n * 4 + u
+                row = ((step - FILLS) * (OWNERS // FILLS) + at) * PITCH
+                for k in range(8):
+                    v = os[k, pl.ds(row, ROWS), :].astype(LOW)
+                    out[at, :, k * 128 : k * 128 + 128] = v
+            return 0
+
+        lax.fori_loop(0, OWNERS // FILLS // 4, gather, 0)
+
+
+def compress_pulses(first, second, third, fourth, turns, xs, os, phase):
     def one(p):
         def load(odd):
             def half(c):
-                at = pl.ds(odd * ROWS + p, 128, stride=2 * ROWS)
+                at = pl.ds(odd * PITCH + p, 128, stride=2 * PITCH)
                 return beside(xs[c, 0, at, :], xs[c, 1, at, :])
 
             return above(half(0), half(1)).astype(LOW)
 
         even = dot(first[0], load(0))
         odd = dot(first[1], load(1))
+        yield 1
         lo, hi = even + odd, even - odd
         parts = [(v[:128], v[128:], slice(r, r + 128)) for v, r in ((lo, 0), (hi, 128))]
         turned = []
@@ -147,59 +202,62 @@
             s = phase[1, :, e * 128 : e * 128 + 128]
             re, im = z[:, :128], z[:, 128:]
             turned.append(beside(re * c - im * s, re * s + im * c).astype(LOW))
+        yield 1
         (r0, i0), (r1, i1) = back_section(turned[0], turned[1], turns, third)
         re, im = beside(r0, r1), beside(i0, i1)
         sums = above(re[:128] + re[128:], im[:128] + im[128:]).astype(LOW)
         gaps = above(re[:128] - re[128:], im[:128] - im[128:]).astype(LOW)
+        yield 1
         for o, c in enumerate((dot(fourth[0], sums), dot(fourth[1], gaps))):
             for part in range(2):
                 for h in range(2):
-                    os[part * 4 + o * 2 + h, pl.ds(p, 128, stride=ROWS), :] = c[
+                    os[part * 4 + o * 2 + h, pl.ds(p, 128, stride=PITCH), :] = c[
                         part * 128 : part * 128 + 128, h * 128 : h * 128 + 128
                     ]
 
-    def pair(i, _):
-        one(2 * i)
-        one(2 * i + 1)
-        return 0
-
-    lax.fori_loop(0, ROWS // 2, pair, 0)
-
-    def gather(n, _):
-        rows = pl.ds(pl.multiple_of(n * 128, 128), 128)
-        for k in range(8):
-            v = os[k, rows, :].astype(LOW).reshape(8, ROWS, 128)
-            out[pl.ds(n * 8, 8), :, k * 128 : k * 128 + 128] = v
-        return 0
-
-    lax.fori_loop(0, 16, gather, 0)
-
-
-def range_compress(raw, phase, tables, turns):
+    def some(i, _):
+        together([one(4 * i + u) for u in range(4)])
+        return 0
+
+    lax.fori_loop(0, ROWS // 4, some, 0)
+
+
+def range_compress(raw, angles, tables, turns):
     return pl.pallas_call(
         compress_kernel,
+        grid=(2 * FILLS,),
+        in_specs=[
+            pl.BlockSpec((2, ROWS, BINS // FILLS), lambda i: (0, 0, jnp.minimum(i, FILLS - 1))),
+            whole((128, 512)),
+            *[whole((2, 256, 256)) for _ in range(5)],
+        ],
+        out_specs=pl.BlockSpec(
+            (OWNERS // FILLS, ROWS, 1024), lambda i: (jnp.maximum(i - FILLS, 0), 0, 0)
+        ),
         out_shape=jax.ShapeDtypeStruct((OWNERS, ROWS, 1024), LOW),
         scratch_shapes=[
-            pltpu.VMEM((2, 2, 256 * ROWS, 128), F32),
-            pltpu.VMEM((8, OWNERS * ROWS, 128), F32),
+            pltpu.VMEM((2, 2, 256 * PITCH, 128), F32),
+            pltpu.VMEM((8, OWNERS * PITCH, 128), F32),
+            pltpu.VMEM((2, 256, 256), F32),
         ],
         name="range_compress",
-    )(raw, phase, *tables, turns)
+    )(raw, angles, *tables, turns)
 
 
 def spread_rows(source, xs):
     def move(n, _):
-        rows = pl.ds(pl.multiple_of(n * 128, 128), 128)
-        for h in range(2):
-            v = source[pl.ds(n * 8, 8), :, h * 128 : h * 128 + 128].astype(F32)
-            xs[h, rows, :] = v.reshape(128, 128)
+        for u in range(8):
+            at = n * 8 + u
+            for h in range(2):
+                v = source[at, :, h * 128 : h * 128 + 128].astype(F32)
+                xs[h, pl.ds(at * PITCH, ROWS), :] = v
         return 0
 
     lax.fori_loop(0, 16, move, 0)
 
 
 def pulse_rows(xs, p):
-    at = pl.ds(p, 128, stride=ROWS)
+    at = pl.ds(p, 128, stride=PITCH)
     return beside(xs[0, at, :], xs[1, at, :])
 
 
@@ -212,7 +270,7 @@
         ys[p] = dot(full[...], x).astype(LOW)
         return 0
 
-    lax.fori_loop(0, 16, outer, 0, unroll=4)
+    lax.fori_loop(0, 16, outer, 0, unroll=8)
 
     def inner(g, _):
         rows = pl.ds(pl.multiple_of(g * 16, 16), 16)
@@ -225,31 +283,28 @@
         vs[:, rows, :] = dot(backward[g], z).astype(LOW).reshape(16, 16, 256)
         return 0
 
-    lax.fori_loop(0, 16, inner, 0, unroll=2)
+    lax.fori_loop(0, 16, inner, 0, unroll=4)
 
     def last(p, _):
         x = dot(back[...], vs[p])
         a, b = x[:128], x[128:]
         m = jnp.sqrt(a * a + b * b)
-        at = pl.ds(p, 128, stride=ROWS)
+        at = pl.ds(p, 128, stride=PITCH)
         ms[0, at, :] = m[:, :128]
         ms[1, at, :] = m[:, 128:]
         return 0
 
-    lax.fori_loop(0, 16, last, 0, unroll=4)
+    lax.fori_loop(0, 16, last, 0, unroll=8)
 
     def gather(n, _):
-        rows = pl.ds(pl.multiple_of(n * 128, 128), 128)
-        for h in range(2):
-            v = ms[h, rows, :].astype(LOW).reshape(8, ROWS, 128)
-            out[pl.ds(n * 8, 8), :, h * 128 : h * 128 + 128] = v
+        for u in range(8):
+            at = n * 8 + u
+            for h in range(2):
+                v = ms[h, pl.ds(at * PITCH, ROWS), :].astype(LOW)
+                out[at, :, h * 128 : h * 128 + 128] = v
         return 0
 
     lax.fori_loop(0, 16, gather, 0)
-
-
-def whole(shape):
-    return pl.BlockSpec(shape, lambda i: (0,) * len(shape))
 
 
 def azimuth_picture(received, phase, full, back, forward, backward):
@@ -268,11 +323,11 @@
         out_specs=pl.BlockSpec((OWNERS, ROWS, 256), lambda i: (0, 0, i)),
         out_shape=jax.ShapeDtypeStruct((OWNERS, ROWS, WIDTH), LOW),
         scratch_shapes=[
-            pltpu.VMEM((2, PULSES, 128), F32),
-            pltpu.VMEM((2, PULSES, 128), F32),
+            pltpu.VMEM((2, OWNERS * PITCH, 128), F32),
+            pltpu.VMEM((2, OWNERS * PITCH, 128), F32),
             pltpu.VMEM((16, 256, 256), LOW),
             pltpu.VMEM((16, 256, 256), LOW),
-            pltpu.VMEM((2, PULSES, 128), F32),
+            pltpu.VMEM((2, OWNERS * PITCH, 128), F32),
         ],
         name="azimuth_picture",
     )(received, received, phase, full, back, forward, backward)
@@ -300,7 +355,7 @@
 
     def last(p, _):
         x = dot(back[:128, :], vs[p])
-        at = pl.ds(p, 128, stride=ROWS)
+        at = pl.ds(p, 128, stride=PITCH)
         ms[0, at, :] = x[:, :128]
         ms[1, at, :] = x[:, 128:]
         return 0
@@ -308,9 +363,11 @@
     lax.fori_loop(0, 16, last, 0, unroll=4)
 
     def gather(n, _):
-        rows = pl.ds(pl.multiple_of(n * 128, 128), 128)
-        out[rows, :128] = ms[0, rows, :]
-        out[rows, 128:] = ms[1, rows, :]
+        for u in range(8):
+            at = n * 8 + u
+            rows = pl.ds(pl.multiple_of(at * ROWS, ROWS), ROWS)
+            for h in range(2):
+                out[rows, h * 128 : h * 128 + 128] = ms[h, pl.ds(at * PITCH, ROWS), :]
         return 0
 
     lax.fori_loop(0, 16, gather, 0)
@@ -331,30 +388,55 @@
         out_specs=pl.BlockSpec((PULSES, 256), lambda i: (0, i)),
         out_shape=jax.ShapeDtypeStruct((PULSES, WIDTH), F32),
         scratch_shapes=[
-            pltpu.VMEM((2, PULSES, 128), F32),
+            pltpu.VMEM((2, OWNERS * PITCH, 128), F32),
             pltpu.VMEM((16, 256, 256), LOW),
             pltpu.VMEM((16, 256, 256), LOW),
-            pltpu.VMEM((2, PULSES, 128), F32),
+            pltpu.VMEM((2, OWNERS * PITCH, 128), F32),
         ],
         name="azimuth_edges",
     )(mag, weights, full, back, forward, backward)
 
 
 def concentrate_kernel(mag, weights, first, second, third, last, turns, out, xs, os):
-    def spread(n, _):
-        rows = pl.ds(pl.multiple_of(n * 128, 128), 128)
-        for k in range(4):
-            v = mag[pl.ds(n * 8, 8), :, k * 128 : k * 128 + 128].astype(F32)
-            xs[k, rows, :] = v.reshape(128, 128)
-        return 0
-
-    lax.fori_loop(0, 16, spread, 0)
+    step = pl.program_id(0)
+
+    @pl.when(step < 2)
+    def _():
+        def spread(n, _):
+            for u in range(4):
+                at = n * 4 + u
+                for k in range(4):
+                    v = mag[at, :, k * 128 : k * 128 + 128].astype(F32)
+                    xs[k, pl.ds((step * (OWNERS // 2) + at) * PITCH, ROWS), :] = v
+            return 0
+
+        lax.fori_loop(0, OWNERS // 8, spread, 0)
+
+    @pl.when(step == 1)
+    def _():
+        concentrate_pulses(weights, first, second, third, last, turns, xs, os)
+
+    @pl.when(step >= 2)
+    def _():
+        def gather(n, _):
+            for u in range(4):
+                at = n * 4 + u
+                rows = pl.ds(((step - 2) * (256 // FILLS) + at) * PITCH, ROWS)
+                lanes = pl.ds(pl.multiple_of(at * 256, 256), 256)
+                out[:, lanes] = beside(os[0, rows, :], os[1, rows, :])
+            return 0
+
+        lax.fori_loop(0, 64 // FILLS, gather, 0)
+
+
+def concentrate_pulses(weights, first, second, third, last, turns, xs, os):
     top = lax.broadcasted_iota(jnp.int32, (128, 256), 0) == 0
 
     def one(p):
-        at = pl.ds(p, 128, stride=ROWS)
+        at = pl.ds(p, 128, stride=PITCH)
         x = above(beside(xs[0, at, :], xs[1, at, :]), beside(xs[2, at, :], xs[3, at, :]))
         y = dot(first[...], x.astype(LOW))
+        yield 1
         re, im = y[:128], y[128:]
         mirror = jnp.where(top[:16], im[:16], 0.0)
         im = jnp.where(top, 0.0, im)
@@ -363,41 +445,45 @@
         for e, z in enumerate(forward_spectrum(parts, turns, second)):
             w = weights[:, e * 128 : e * 128 + 128]
             jumped.append(beside(-z[:, 128:] * w, z[:, :128] * w).astype(LOW))
+        yield 1
         (r0, i0), (r1, i1) = back_section(jumped[0], jumped[1], turns, third)
         re, im = beside(r0, r1), beside(i0, i1)
         im = above(jnp.where(top[:8], re[128:136], im[:8]), im[8:128])
+        yield 1
         e = dot(last[...], above(re[:128], im).astype(LOW))
         for o in range(2):
             for h in range(2):
-                os[h, pl.ds(o * ROWS + p, 128, stride=2 * ROWS), :] = e[
+                os[h, pl.ds(o * PITCH + p, 128, stride=2 * PITCH), :] = e[
                     o * 128 : o * 128 + 128, h * 128 : h * 128 + 128
                 ]
 
-    def pair(i, _):
-        one(2 * i)
-        one(2 * i + 1)
-        return 0
-
-    lax.fori_loop(0, ROWS // 2, pair, 0)
-
-    def gather(n, _):
-        for u in range(4):
-            at = n * 4 + u
-            rows = pl.ds(pl.multiple_of(at * ROWS, ROWS), ROWS)
-            out[:, pl.ds(pl.multiple_of(at * 256, 256), 256)] = beside(os[0, rows, :], os[1, rows, :])
-        return 0
-
-    lax.fori_loop(0, 64, gather, 0)
+    def some(i, _):
+        together([one(4 * i + u) for u in range(4)])
+        return 0
+
+    lax.fori_loop(0, ROWS // 4, some, 0)
 
 
 def range_concentrate(mag, weights, first, second, third, last, turns):
     return pl.pallas_call(
         concentrate_kernel,
+        grid=(2 + FILLS,),
+        in_specs=[
+            pl.BlockSpec((OWNERS // 2, ROWS, WIDTH), lambda i: (jnp.minimum(i, 1), 0, 0)),
+            whole((144, 256)),
+            whole((256, 256)),
+            whole((2, 256, 256)),
+            whole((2, 256, 256)),
+            whole((256, 256)),
+            whole((2, 256, 256)),
+        ],
+        out_specs=pl.BlockSpec((ROWS, BINS // FILLS), lambda i: (0, jnp.maximum(i - 2, 0))),
         out_shape=jax.ShapeDtypeStruct((ROWS, BINS), F32),
         scratch_shapes=[
-            pltpu.VMEM((4, PULSES, 128), F32),
-            pltpu.VMEM((2, 256 * ROWS, 128), F32),
-        ],
+            pltpu.VMEM((4, OWNERS * PITCH, 128), F32),
+            pltpu.VMEM((2, 256 * PITCH, 128), F32),
+        ],
+        compiler_params=pltpu.CompilerParams(vmem_limit_bytes=32 << 20),
         name="range_concentrate",
     )(mag, weights, first, second, third, last, turns)
 
@@ -444,9 +530,8 @@
 def on_device(raw_pulses, range_phase, azimuth_rate, conc_azimuth, conc_range):
     first, second, third, fourth = range_tables()
     turns = jnp.asarray(range_turns(256))
-    grid = split_grid(range_phase)
-    phase = jnp.stack([jnp.cos(grid), jnp.sin(grid)])
-    blocks = range_compress(raw_pulses, phase, (first, second, third, fourth), turns)
+    angles = range_phase.reshape(128, 512)
+    blocks = range_compress(raw_pulses, angles, (first, second, third, fourth), turns)
     received = lax.all_to_all(blocks, AXES, split_axis=0, concat_axis=0, tiled=True)
     full, back, forward, backward = azimuth_tables()
     forward, backward, _ = lax.optimization_barrier((forward, backward, conc_azimuth))

time: 169 us -> 138 us (0.82)
  Pallas kernels: 82.3 us -> 53.5 us
  local copies, waits for them, and re-layouts: 8.16 us -> 4.98 us
  waiting for transfers between devices: 36.4 us -> 38.1 us
    pallas_call x2, Pallas kernels: 42.4 us -> 20.9 us  [the longest x1 13.9 us: range_compress(): pl.pallas_call(compress_kernel, grid=(2 * FILLS,), in_specs=[pl.BlockSpec...]
    pallas_call x1, Pallas kernels: 21.8 us -> 15.6 us  [azimuth_picture(): pl.pallas_call(picture_kernel, grid=(2,), in_specs=[pl.BlockSpec((OWNERS,...]
    cos x4 -> x0, local copies, waits for them, and re-layouts: 2.39 us -> none  [on_device(): phase = jnp.stack([jnp.cos(grid), jnp.sin(grid)])]
    unnamed x15 -> x23, local copies, waits for them, and re-layouts: 2.53 us -> 0.57 us
    all_to_all x1, waiting for transfers between devices: 6.92 us -> 8.65 us  [on_device(): shared = lax.all_to_all(mag, AXES, split_axis=0, concat_axis=0, tiled=True)]
    reshape x0 -> x1, local copies, waits for them, and re-layouts: none -> 1.69 us  [on_device(): angles = range_phase.reshape(128, 512)]
  transfers between devices with their start and end apart: 2 -> 2, of which waited for: 2 -> 2; matrix products, arithmetic and copies ran while one was open for 16% -> 19% of each run, Pallas kernels for 11% -> 12%
where the time goes in v1:
time: 138 us; the launch traced here: 137 us
  Pallas kernels  53.5 us (39%)
  waiting for transfers between devices  38.1 us (28%)
  other arithmetic  22.3 us (16%)
  starting transfers between devices  17.8 us (13%)
  local copies, waits for them, and re-layouts  4.98 us (4%)
    all_to_all x1, waiting for transfers between devices, on_device(): lax.all_to_all(blocks, AXES, split_axis=0, concat_axis=0, tiled=True)  29.4 us
    pallas_call x1, Pallas kernels, azimuth_edges(): pl.pallas_call(edge_kernel, grid=(2,), in_specs=[pl.BlockSpec((OWNERS, RO...  17 us
    pallas_call x1, Pallas kernels, azimuth_picture(): pl.pallas_call(picture_kernel, grid=(2,), in_specs=[pl.BlockSpec((OWNERS,...  15.6 us
    cos x1, other arithmetic, azimuth_phase(): return jnp.stack([jnp.cos(angles), jnp.sin(angles)])  14.7 us
    pallas_call x1, Pallas kernels, range_compress(): pl.pallas_call(compress_kernel, grid=(2 * FILLS,), in_specs=[pl.BlockSpec...  13.9 us
    all_to_all x1, starting transfers between devices, on_device(): lax.all_to_all(blocks, AXES, split_axis=0, concat_axis=0, tiled=True)  11.9 us
    all_to_all x1, waiting for transfers between devices, on_device(): shared = lax.all_to_all(mag, AXES, split_axis=0, concat_axis=0, tiled=True)  8.65 us
    pallas_call x1, Pallas kernels, range_concentrate(): pl.pallas_call(concentrate_kernel, grid=(2 + FILLS,), in_specs=[pl.BlockS...  7.06 us
  transfers between devices with their start and end apart: 2, of which 2 were waited for; matrix products, arithmetic and copies ran while one was open for 19% of the time, Pallas kernels for 12%

profile of v1, /device:TPU:0, one launch (start us, length us, event | category | flops | bytes accessed | tf_op | source)
XLA Modules:
  0.0 137.5 jit_solution(12831302764998979661)
XLA Ops:
  0.6 1.7 %reshape.153.angles = f32[128,512]{1,0:T(8,128)} reshape(f32[65536]{0:T(1024)} %param.17) | data formatting | bytes 524288 | tf_op jit(solution)/shard_map/reshape | solution.py:533
  2.3 13.9 %range_compress.1 = bf16[128,16,1024]{2,1,0:T(8,128)(2,1)} custom-call(bf16[2,16,65536]{2,1,0:T(8,128)(2,1)} %raw.1, f32[128,512]{1,0:T(8,128)} %reshape.153.angles, bf16[2,256,256]{2,1,0:T(8,128)(2,1)} %constant.78.clone.first, bf16[2,256,256]{2,1,0:T(8,128)(2,1)} %constant.79.clone.second, bf16[2,256,256]{2,1,0:T(8,128)(2,1)} %constant.80.clone.third, ...), custom_call_target="tpu_custom_call" | custom-call | tf_op jit(solution)/shard_map/range_compress/pallas_call | solution.py:226
  16.2 0.0 copy-start.9
  16.2 11.9 %all-to-all-start = ((bf16[128,16,1024]{2,1,0:T(8,128)(2,1)}), bf16[128,16,1024]{2,1,0:T(8,128)(2,1)}, u32[]{:S(2)}, u32[]{:S(2)}) async-start(bf16[128,16,1024]{2,1,0:T(8,128)(2,1)} %range_compress.1), calls=%async_computation | async-start | bytes 8388608 | tf_op jit(solution)/shard_map/all_to_all | solution.py:535
  28.1 0.1 reshape.159
  28.2 0.1 iota.64
  28.4 0.0 copy-done.9
  28.4 14.7 %multiply_cosine_fusion = (f32[1,16,128,512]{3,2,1,0:T(8,128)S(1)}, f32[1,16,128,512]{3,2,1,0:T(8,128)S(1)}) fusion(f32[512]{0:T(512)S(1)} %copy-done.9, f32[16,128]{1,0:T(8,128)S(1)} %fusion.9), kind=kLoop, calls=%fused_computation.2 | loop fusion | flops 1048576 | bytes 8398848 | tf_op jit(solution)/shard_map/cos | solution.py:504
  43.1 0.0 copy-start.6
  43.1 0.0 copy-start.7
  43.1 4.3 %pad_maximum_fusion.phase = f32[2,16,128,512]{3,2,1,0:T(8,128)} fusion(f32[1,16,128,512]{3,2,1,0:T(8,128)S(1)} %get-tuple-element.9, f32[1,16,128,512]{3,2,1,0:T(8,128)S(1)} %get-tuple-element.8), kind=kLoop, calls=%fused_computation | loop fusion | flops 2097152 | bytes 16777216 | tf_op jit(solution)/shard_map/stack | solution.py:504
  47.4 0.0 copy-done.6
  47.4 0.0 copy-done.7
  47.4 2.5 %bitcast_select_fusion = (bf16[16,256,256]{2,1,0:T(8,128)(2,1)}, bf16[16,256,256]{2,1,0:T(8,128)(2,1)}) fusion(pred[256,256]{1,0:T(8,128)(4,1)S(1)} %broadcast_bitcast_fusion, bf16[16,32,256]{2,1,0:T(8,128)(2,1)S(1)} %copy-done.7, bf16[16,32,256]{2,1,0:T(8,128)(2,1)S(1)} %copy-done.6), kind=kLoop, calls=%fused_computation.3 | loop fusion | flops 2097152 | bytes 4784128 | tf_op jit(solution)/shard_map/jit(_where)/select_n | solution.py:526
  49.9 29.4 %all-to-all-done.re.im = bf16[128,16,1024]{2,1,0:T(8,128)(2,1)} async-done(((bf16[128,16,1024]{2,1,0:T(8,128)(2,1)}), bf16[128,16,1024]{2,1,0:T(8,128)(2,1)}, u32[]{:S(2)}, u32[]{:S(2)}) %all-to-all-start) | async-done | bytes 4194336 | tf_op jit(solution)/shard_map/all_to_all | solution.py:535
  79.3 15.6 %azimuth_picture.1.mag = bf16[128,16,512]{2,1,0:T(8,128)(2,1)} custom-call(bf16[128,16,1024]{2,1,0:T(8,128)(2,1)} %all-to-all-done.re.im, bf16[128,16,1024]{2,1,0:T(8,128)(2,1)} %all-to-all-done.re.im, f32[2,16,128,512]{3,2,1,0:T(8,128)} %pad_maximum_fusion.phase, bf16[256,256]{1,0:T(8,128)(2,1)} %constant.84.clone.full, ...), custom_call_target="tpu_custom_call" | custom-call | tf_op jit(solution)/shard_map/azimuth_picture/pallas_call | solution.py:311
  94.9 0.0 copy-start.5
  94.9 0.0 copy-start.8
  94.9 5.9 %all-to-all-start.1 = ((bf16[128,16,512]{2,1,0:T(8,128)(2,1)}), bf16[128,16,512]{2,1,0:T(8,128)(2,1)S(1)}, u32[]{:S(2)}, u32[]{:S(2)}) async-start(bf16[128,16,512]{2,1,0:T(8,128)(2,1)} %azimuth_picture.1.mag), calls=%async_computation.1 | async-start | bytes 4194304 | tf_op jit(solution)/shard_map/all_to_all | solution.py:541
  100.8 0.0 copy-done.5
  100.8 0.1 slice.19
  101.0 0.5 slice.18
  101.5 0.0 copy-done.8
  101.5 0.1 reshape.161
  101.6 0.1 copy.18
  101.7 0.1 copy.19
  101.8 0.4 reverse.2
  102.1 0.1 slice.24
  102.3 0.8 fusion.1
  103.1 0.2 reshape.162
  103.2 0.2 copy.20
  103.4 1.3 broadcast_in_dim.62.weights
  104.7 0.0 copy-start
  104.7 0.0 copy-start.1
  104.7 0.0 copy-start.2
  104.7 0.0 copy-start.3
  104.7 0.0 copy-start.4
  104.8 17.0 %azimuth_edges.1 = f32[2048,512]{1,0:T(8,128)} custom-call(bf16[128,16,512]{2,1,0:T(8,128)(2,1)} %azimuth_picture.1.mag, f32[16,128,128]{2,1,0:T(8,128)} %broadcast_in_dim.62.weights, bf16[256,256]{1,0:T(8,128)(2,1)} %constant.84.clone.full, bf16[256,256]{1,0:T(8,128)(2,1)} %constant.85.clone.back, bf16[16,256,256]{2,1,0:T(8,128)(2,1)} %get-tuple-element.7.forward, ...), custom_call_target="tpu_custom_call" | custom-call | tf_op jit(solution)/shard_map/azimuth_edges/pallas_call | solution.py:377
  121.7 8.6 %all-to-all-done.1.mag = bf16[128,16,512]{2,1,0:T(8,128)(2,1)S(1)} async-done(((bf16[128,16,512]{2,1,0:T(8,128)(2,1)}), bf16[128,16,512]{2,1,0:T(8,128)(2,1)S(1)}, u32[]{:S(2)}, u32[]{:S(2)}) %all-to-all-start.1) | async-done | bytes 2097184 | tf_op jit(solution)/shard_map/all_to_all | solution.py:541
  130.4 0.0 copy-done
  130.4 0.0 copy-done.1
  130.4 0.0 copy-done.2
  130.4 0.0 copy-done.3
  130.4 0.0 copy-done.4
  130.4 7.1 %range_concentrate.1 = f32[16,65536]{1,0:T(8,128)} custom-call(bf16[128,16,512]{2,1,0:T(8,128)(2,1)S(1)} %all-to-all-done.1.mag, f32[144,256]{1,0:T(8,128)S(1)} %bitcast.15, bf16[256,256]{1,0:T(8,128)(2,1)S(1)} %copy-done.3, bf16[2,256,256]{2,1,0:T(8,128)(2,1)S(1)} %copy-done.1, bf16[2,256,256]{2,1,0:T(8,128)(2,1)S(1)} %copy-done.2, ...), custom_call_target="tpu_custom_call" | custom-call | tf_op jit(solution)/shard_map/range_concentrate/pallas_call | solution.py:468
  (9 shorter events, 0.1 us)
Async XLA Ops:
  16.2 12.2 %copy-start.9 = (f32[512]{0:T(512)S(1)}, f32[512]{0:T(512)}, u32[]{:S(2)}) copy-start(f32[512]{0:T(512)} %param.18) | copy-start | bytes 6148
  16.2 63.2 %all-to-all-start = ((bf16[128,16,1024]{2,1,0:T(8,128)(2,1)}), bf16[128,16,1024]{2,1,0:T(8,128)(2,1)}, u32[]{:S(2)}, u32[]{:S(2)}) async-start(bf16[128,16,1024]{2,1,0:T(8,128)(2,1)} %range_compress.1), calls=%async_computation | async-start | bytes 8388608 | tf_op jit(solution)/shard_map/all_to_all | solution.py:535
  43.1 4.3 %copy-start.6 = (bf16[16,32,256]{2,1,0:T(8,128)(2,1)S(1)}, bf16[16,32,256]{2,1,0:T(8,128)(2,1)}, u32[]{:S(2)}) copy-start(bf16[16,32,256]{2,1,0:T(8,128)(2,1)} %constant.82.clone) | copy-start | bytes 786436
  43.1 4.3 %copy-start.7 = (bf16[16,32,256]{2,1,0:T(8,128)(2,1)S(1)}, bf16[16,32,256]{2,1,0:T(8,128)(2,1)}, u32[]{:S(2)}) copy-start(bf16[16,32,256]{2,1,0:T(8,128)(2,1)} %constant.83.clone) | copy-start | bytes 786436
  94.9 5.9 %copy-start.5 = (f32[65536]{0:T(1024)S(1)}, f32[65536]{0:T(1024)}, u32[]{:S(2)}) copy-start(f32[65536]{0:T(1024)} %param.20) | copy-start | bytes 786436
  94.9 6.6 %copy-start.8 = (f32[2048]{0:T(1024)S(1)}, f32[2048]{0:T(1024)}, u32[]{:S(2)}) copy-start(f32[2048]{0:T(1024)} %param.19) | copy-start | bytes 24580
  94.9 35.5 %all-to-all-start.1 = ((bf16[128,16,512]{2,1,0:T(8,128)(2,1)}), bf16[128,16,512]{2,1,0:T(8,128)(2,1)S(1)}, u32[]{:S(2)}, u32[]{:S(2)}) async-start(bf16[128,16,512]{2,1,0:T(8,128)(2,1)} %azimuth_picture.1.mag), calls=%async_computation.1 | async-start | bytes 4194304 | tf_op jit(solution)/shard_map/all_to_all | solution.py:541
  104.7 25.7 %copy-start = (f32[2,256,256]{2,1,0:T(8,128)S(1)}, f32[2,256,256]{2,1,0:T(8,128)}, u32[]{:S(2)}) copy-start(f32[2,256,256]{2,1,0:T(8,128)} %constant.77.clone.turns) | copy-start | bytes 1572868
  104.7 25.7 %copy-start.1 = (bf16[2,256,256]{2,1,0:T(8,128)(2,1)S(1)}, bf16[2,256,256]{2,1,0:T(8,128)(2,1)}, u32[]{:S(2)}) copy-start(bf16[2,256,256]{2,1,0:T(8,128)(2,1)} %constant.79.clone.second) | copy-start | bytes 786436
  104.7 25.7 %copy-start.2 = (bf16[2,256,256]{2,1,0:T(8,128)(2,1)S(1)}, bf16[2,256,256]{2,1,0:T(8,128)(2,1)}, u32[]{:S(2)}) copy-start(bf16[2,256,256]{2,1,0:T(8,128)(2,1)} %constant.80.clone.third) | copy-start | bytes 786436
  104.7 25.7 %copy-start.3 = (bf16[256,256]{1,0:T(8,128)(2,1)S(1)}, bf16[256,256]{1,0:T(8,128)(2,1)}, u32[]{:S(2)}) copy-start(bf16[256,256]{1,0:T(8,128)(2,1)} %constant.86.clone.first) | copy-start | bytes 393220
  104.7 25.7 %copy-start.4 = (bf16[256,256]{1,0:T(8,128)(2,1)S(1)}, bf16[256,256]{1,0:T(8,128)(2,1)}, u32[]{:S(2)}) copy-start(bf16[256,256]{1,0:T(8,128)(2,1)} %constant.87.clone.last) | copy-start | bytes 393220

commit v2 on v1

--- a/solution.py
+++ b/solution.py
@@ -13,6 +13,7 @@
 PULSES = 2048
 ROWS = 16
 PITCH = 18
+SMALLEST = float(np.finfo(np.float32).tiny)
 FILLS = 4
 OWNERS = 128
 WIDTH = 512
@@ -145,16 +146,18 @@
 
     @pl.when(step == 0)
     def _():
-        sine, cosine = sine_cosine(angles[...].T)
         for e in range(2):
-            phase[0, :, e * 128 : e * 128 + 128] = cosine[e * 256 : e * 256 + 256]
-            phase[1, :, e * 128 : e * 128 + 128] = sine[e * 256 : e * 256 + 256]
+            for h in range(2):
+                part = angles[pl.ds(2 * e + h, 128, stride=4), :]
+                sine, cosine = sine_cosine(part.T)
+                phase[0, h * 128 : h * 128 + 128, e * 128 : e * 128 + 128] = cosine
+                phase[1, h * 128 : h * 128 + 128, e * 128 : e * 128 + 128] = sine
 
     @pl.when(step < FILLS)
     def _():
         def spread(n, _):
-            for u in range(4):
-                at = n * 4 + u
+            for u in range(8):
+                at = n * 8 + u
                 for c in range(2):
                     v = raw[c, :, pl.ds(pl.multiple_of(at * 256, 256), 256)].astype(F32)
                     row = (step * (256 // FILLS) + at) * PITCH
@@ -162,7 +165,7 @@
                     xs[c, 1, pl.ds(row, ROWS), :] = v[:, 128:]
             return 0
 
-        lax.fori_loop(0, 64 // FILLS, spread, 0)
+        lax.fori_loop(0, 32 // FILLS, spread, 0)
 
     @pl.when(step == FILLS - 1)
     def _():
@@ -176,7 +179,7 @@
                 row = ((step - FILLS) * (OWNERS // FILLS) + at) * PITCH
                 for k in range(8):
                     v = os[k, pl.ds(row, ROWS), :].astype(LOW)
-                    out[at, :, k * 128 : k * 128 + 128] = v
+                    out[at, k] = v
             return 0
 
         lax.fori_loop(0, OWNERS // FILLS // 4, gather, 0)
@@ -228,13 +231,13 @@
         grid=(2 * FILLS,),
         in_specs=[
             pl.BlockSpec((2, ROWS, BINS // FILLS), lambda i: (0, 0, jnp.minimum(i, FILLS - 1))),
-            whole((128, 512)),
+            whole((512, 128)),
             *[whole((2, 256, 256)) for _ in range(5)],
         ],
         out_specs=pl.BlockSpec(
-            (OWNERS // FILLS, ROWS, 1024), lambda i: (jnp.maximum(i - FILLS, 0), 0, 0)
+            (OWNERS // FILLS, 8, ROWS, 128), lambda i: (jnp.maximum(i - FILLS, 0), 0, 0, 0)
         ),
-        out_shape=jax.ShapeDtypeStruct((OWNERS, ROWS, 1024), LOW),
+        out_shape=jax.ShapeDtypeStruct((OWNERS, 8, ROWS, 128), LOW),
         scratch_shapes=[
             pltpu.VMEM((2, 2, 256 * PITCH, 128), F32),
             pltpu.VMEM((8, OWNERS * PITCH, 128), F32),
@@ -249,7 +252,7 @@
         for u in range(8):
             at = n * 8 + u
             for h in range(2):
-                v = source[at, :, h * 128 : h * 128 + 128].astype(F32)
+                v = source[at, h].astype(F32)
                 xs[h, pl.ds(at * PITCH, ROWS), :] = v
         return 0
 
@@ -261,7 +264,25 @@
     return beside(xs[0, at, :], xs[1, at, :])
 
 
-def picture_kernel(re, im, phase, full, back, forward, backward, out, xr, xi, ys, vs, ms):
+def picture_kernel(
+    re, im, cosine_far, sine_far, full, back, forward_far, backward_far, out,
+    xr, xi, ys, vs, ms, cosine, sine, forward, backward, arrived,
+):
+    step = pl.program_id(0)
+    tables = [
+        pltpu.make_async_copy(forward_far, forward, arrived.at[0]),
+        pltpu.make_async_copy(cosine_far.at[0], cosine.at[0], arrived.at[1]),
+        pltpu.make_async_copy(sine_far.at[0], sine.at[0], arrived.at[2]),
+        pltpu.make_async_copy(backward_far, backward, arrived.at[3]),
+        pltpu.make_async_copy(cosine_far.at[1], cosine.at[1], arrived.at[4]),
+        pltpu.make_async_copy(sine_far.at[1], sine.at[1], arrived.at[5]),
+    ]
+
+    @pl.when(step == 0)
+    def _():
+        for table in tables:
+            table.start()
+
     spread_rows(re, xr)
     spread_rows(im, xi)
 
@@ -272,11 +293,21 @@
 
     lax.fori_loop(0, 16, outer, 0, unroll=8)
 
+    @pl.when(step == 0)
+    def _():
+        for table in tables[:4]:
+            table.wait()
+
+    @pl.when(step == 1)
+    def _():
+        for table in tables[4:]:
+            table.wait()
+
     def inner(g, _):
         rows = pl.ds(pl.multiple_of(g * 16, 16), 16)
         y = dot(forward[g], ys[:, rows, :].reshape(256, 256)).reshape(16, 2, 8, 256)
-        c = phase[0, g].reshape(16, 8, 256)
-        s = phase[1, g].reshape(16, 8, 256)
+        c = cosine[step, g].reshape(16, 8, 256)
+        s = sine[step, g].reshape(16, 8, 256)
         zr = y[:, 0] * c - y[:, 1] * s
         zi = y[:, 0] * s + y[:, 1] * c
         z = jnp.stack([zr, zi], 1).reshape(256, 256).astype(LOW)
@@ -288,7 +319,8 @@
     def last(p, _):
         x = dot(back[...], vs[p])
         a, b = x[:128], x[128:]
-        m = jnp.sqrt(a * a + b * b)
+        m = a * a + b * b
+        m = m * lax.rsqrt(jnp.maximum(m, SMALLEST))
         at = pl.ds(p, 128, stride=PITCH)
         ms[0, at, :] = m[:, :128]
         ms[1, at, :] = m[:, 128:]
@@ -300,37 +332,42 @@
         for u in range(8):
             at = n * 8 + u
             for h in range(2):
-                v = ms[h, pl.ds(at * PITCH, ROWS), :].astype(LOW)
-                out[at, :, h * 128 : h * 128 + 128] = v
+                out[at, h] = ms[h, pl.ds(at * PITCH, ROWS), :].astype(LOW)
         return 0
 
     lax.fori_loop(0, 16, gather, 0)
 
 
-def azimuth_picture(received, phase, full, back, forward, backward):
+def azimuth_picture(received, cosine, sine, full, back, forward, backward):
     return pl.pallas_call(
         picture_kernel,
         grid=(2,),
         in_specs=[
-            pl.BlockSpec((OWNERS, ROWS, 256), lambda i: (0, 0, i)),
-            pl.BlockSpec((OWNERS, ROWS, 256), lambda i: (0, 0, i + 2)),
-            pl.BlockSpec((2, 16, 128, 256), lambda i: (0, 0, 0, i)),
+            pl.BlockSpec((OWNERS, 2, ROWS, 128), lambda i: (0, i, 0, 0)),
+            pl.BlockSpec((OWNERS, 2, ROWS, 128), lambda i: (0, i + 2, 0, 0)),
+            pl.BlockSpec(memory_space=pltpu.HBM),
+            pl.BlockSpec(memory_space=pltpu.HBM),
             whole((256, 256)),
             whole((256, 256)),
-            whole((16, 256, 256)),
-            whole((16, 256, 256)),
-        ],
-        out_specs=pl.BlockSpec((OWNERS, ROWS, 256), lambda i: (0, 0, i)),
-        out_shape=jax.ShapeDtypeStruct((OWNERS, ROWS, WIDTH), LOW),
+            pl.BlockSpec(memory_space=pltpu.HBM),
+            pl.BlockSpec(memory_space=pltpu.HBM),
+        ],
+        out_specs=pl.BlockSpec((OWNERS, 2, ROWS, 128), lambda i: (0, i, 0, 0)),
+        out_shape=pltpu.HBM((OWNERS, 4, ROWS, 128), LOW),
         scratch_shapes=[
             pltpu.VMEM((2, OWNERS * PITCH, 128), F32),
             pltpu.VMEM((2, OWNERS * PITCH, 128), F32),
             pltpu.VMEM((16, 256, 256), LOW),
             pltpu.VMEM((16, 256, 256), LOW),
             pltpu.VMEM((2, OWNERS * PITCH, 128), F32),
+            pltpu.VMEM((2, 16, 128, 256), F32),
+            pltpu.VMEM((2, 16, 128, 256), F32),
+            pltpu.VMEM((16, 256, 256), LOW),
+            pltpu.VMEM((16, 256, 256), LOW),
+            pltpu.SemaphoreType.DMA((6,)),
         ],
         name="azimuth_picture",
-    )(received, received, phase, full, back, forward, backward)
+    )(received, received, cosine, sine, full, back, forward, backward)
 
 
 def edge_kernel(mag, weights, full, back, forward, backward, out, xs, ys, vs, ms):
@@ -378,7 +415,7 @@
         edge_kernel,
         grid=(2,),
         in_specs=[
-            pl.BlockSpec((OWNERS, ROWS, 256), lambda i: (0, 0, i)),
+            pl.BlockSpec((OWNERS, 2, ROWS, 128), lambda i: (0, i, 0, 0)),
             whole((16, 128, 128)),
             whole((256, 256)),
             whole((256, 256)),
@@ -406,7 +443,7 @@
             for u in range(4):
                 at = n * 4 + u
                 for k in range(4):
-                    v = mag[at, :, k * 128 : k * 128 + 128].astype(F32)
+                    v = mag[at, k].astype(F32)
                     xs[k, pl.ds((step * (OWNERS // 2) + at) * PITCH, ROWS), :] = v
             return 0
 
@@ -469,7 +506,7 @@
         concentrate_kernel,
         grid=(2 + FILLS,),
         in_specs=[
-            pl.BlockSpec((OWNERS // 2, ROWS, WIDTH), lambda i: (jnp.minimum(i, 1), 0, 0)),
+            pl.BlockSpec((OWNERS // 2, 4, ROWS, 128), lambda i: (jnp.minimum(i, 1), 0, 0, 0)),
             whole((144, 256)),
             whole((256, 256)),
             whole((2, 256, 256)),
@@ -499,9 +536,9 @@
 
 def azimuth_phase(rates):
     freqs = jnp.arange(PULSES, dtype=jnp.int32).reshape(16, 16, 8).transpose(1, 0, 2)
-    s = signed(freqs, PULSES).astype(F32).reshape(16, 128, 1) / PULSES
-    angles = (s * s) * rates[None, None, :]
-    return jnp.stack([jnp.cos(angles), jnp.sin(angles)])
+    s = signed(freqs, PULSES).astype(F32).reshape(1, 16, 128, 1) / PULSES
+    angles = (s * s) * rates.reshape(2, 1, 1, 256)
+    return jnp.cos(angles), jnp.sin(angles)
 
 
 def azimuth_weights(factors):
@@ -530,14 +567,14 @@
 def on_device(raw_pulses, range_phase, azimuth_rate, conc_azimuth, conc_range):
     first, second, third, fourth = range_tables()
     turns = jnp.asarray(range_turns(256))
-    angles = range_phase.reshape(128, 512)
+    angles = range_phase.reshape(512, 128)
     blocks = range_compress(raw_pulses, angles, (first, second, third, fourth), turns)
     received = lax.all_to_all(blocks, AXES, split_axis=0, concat_axis=0, tiled=True)
     full, back, forward, backward = azimuth_tables()
     forward, backward, _ = lax.optimization_barrier((forward, backward, conc_azimuth))
     forward, backward = expand(forward), expand(backward)
-    turn = azimuth_phase(azimuth_rate)
-    mag = azimuth_picture(received, turn, full, back, forward, backward)
+    cosine, sine = azimuth_phase(azimuth_rate)
+    mag = azimuth_picture(received, cosine, sine, full, back, forward, backward)
     shared = lax.all_to_all(mag, AXES, split_axis=0, concat_axis=0, tiled=True)
     edge_azimuth = azimuth_edges(mag, azimuth_weights(conc_azimuth), full, back, forward, backward)
     real_first, real_last = real_range_tables()

time: 138 us -> 135 us (0.978)
  waiting for transfers between devices: 38.1 us -> 40.5 us
  other arithmetic: 22.3 us -> 20.3 us
  local copies, waits for them, and re-layouts: 4.98 us -> 3.3 us
    sin x0 -> x1, other arithmetic: none -> 16.9 us  [azimuth_phase(): return (jnp.cos(angles), jnp.sin(angles))]
    cos x1 -> x0, other arithmetic: 14.7 us -> none  [azimuth_phase(): return jnp.stack([jnp.cos(angles), jnp.sin(angles)])]
    another operation x1 -> x0, other arithmetic: 4.25 us -> none  [azimuth_phase(): return jnp.stack([jnp.cos(angles), jnp.sin(angles)])]
    all_to_all x1, waiting for transfers between devices: 29.4 us -> 31.7 us  [on_device(): lax.all_to_all(blocks, AXES, split_axis=0, concat_axis=0, tiled=True)]
    reshape x1 -> x0, local copies, waits for them, and re-layouts: 1.69 us -> none  [on_device(): angles = range_phase.reshape(128, 512)]
  transfers between devices with their start and end apart: 2 -> 2, of which waited for: 2 -> 2; matrix products, arithmetic and copies ran while one was open for 19% -> 17% of each run, Pallas kernels for 12% -> 13%
where the time goes in v2:
time: 135 us
  Pallas kernels  52.4 us (39%)
  waiting for transfers between devices  40.5 us (30%)
  other arithmetic  20.3 us (15%)
  starting transfers between devices  17.4 us (13%)
  local copies, waits for them, and re-layouts  3.3 us (2%)
    all_to_all x1, waiting for transfers between devices, on_device(): lax.all_to_all(blocks, AXES, split_axis=0, concat_axis=0, tiled=True)  31.7 us
    pallas_call x1, Pallas kernels, azimuth_edges(): pl.pallas_call(edge_kernel, grid=(2,), in_specs=[pl.BlockSpec((OWNERS, 2,...  17 us
    sin x1, other arithmetic, azimuth_phase(): return (jnp.cos(angles), jnp.sin(angles))  16.9 us
    pallas_call x1, Pallas kernels, azimuth_picture(): pl.pallas_call(picture_kernel, grid=(2,), in_specs=[pl.BlockSpec((OWNERS,...  14.6 us
    pallas_call x1, Pallas kernels, range_compress(): pl.pallas_call(compress_kernel, grid=(2 * FILLS,), in_specs=[pl.BlockSpec...  13.7 us
    all_to_all x1, starting transfers between devices, on_device(): lax.all_to_all(blocks, AXES, split_axis=0, concat_axis=0, tiled=True)  11.7 us
    all_to_all x1, waiting for transfers between devices, on_device(): shared = lax.all_to_all(mag, AXES, split_axis=0, concat_axis=0, tiled=True)  8.83 us
    pallas_call x1, Pallas kernels, range_concentrate(): pl.pallas_call(concentrate_kernel, grid=(2 + FILLS,), in_specs=[pl.BlockS...  7.06 us
  transfers between devices with their start and end apart: 2, of which 2 were waited for; matrix products, arithmetic and copies ran while one was open for 17% of the time, Pallas kernels for 13%

profile of v2, /device:TPU:0, one launch (start us, length us, event | category | flops | bytes accessed | tf_op | source)
XLA Modules:
  0.0 134.7 jit_solution(869970798895138617)
XLA Ops:
  0.6 13.7 %range_compress.1 = bf16[128,8,16,128]{3,2,1,0:T(8,128)(2,1)} custom-call(bf16[2,16,65536]{2,1,0:T(8,128)(2,1)} %raw.1, f32[512,128]{1,0:T(8,128)} %bitcast.21, bf16[2,256,256]{2,1,0:T(8,128)(2,1)} %constant.78.clone.first, bf16[2,256,256]{2,1,0:T(8,128)(2,1)} %constant.79.clone.second, bf16[2,256,256]{2,1,0:T(8,128)(2,1)} %constant.80.clone.third, ...), custom_call_target="tpu_custom_call" | custom-call | tf_op jit(solution)/shard_map/range_compress/pallas_call | solution.py:229
  14.4 0.0 copy-start.9
  14.4 0.0 copy-start.6
  14.4 0.0 copy-start.7
  14.4 11.7 %all-to-all-start = ((bf16[128,8,16,128]{3,2,1,0:T(8,128)(2,1)}), bf16[128,8,16,128]{3,2,1,0:T(8,128)(2,1)}, u32[]{:S(2)}, u32[]{:S(2)}) async-start(bf16[128,8,16,128]{3,2,1,0:T(8,128)(2,1)} %range_compress.1), calls=%async_computation | async-start | bytes 8388608 | tf_op jit(solution)/shard_map/all_to_all | solution.py:572
  26.1 0.0 copy-done.9
  26.1 0.1 reshape.152
  26.2 0.1 iota.64
  26.4 0.0 copy-done.6
  26.4 0.0 copy-done.7
  26.4 2.6 %bitcast_select_fusion = (bf16[16,256,256]{2,1,0:T(8,128)(2,1)}, bf16[16,256,256]{2,1,0:T(8,128)(2,1)}) fusion(pred[256,256]{1,0:T(8,128)(4,1)S(1)} %broadcast_bitcast_fusion, bf16[16,32,256]{2,1,0:T(8,128)(2,1)S(1)} %copy-done.7, bf16[16,32,256]{2,1,0:T(8,128)(2,1)S(1)} %copy-done.6), kind=kLoop, calls=%fused_computation.2 | loop fusion | flops 2097152 | bytes 4784128 | tf_op jit(solution)/shard_map/jit(_where)/select_n | solution.py:563
  29.0 16.9 %multiply_sine_fusion = (f32[2,16,128,256]{3,2,1,0:T(8,128)}, f32[2,16,128,256]{3,2,1,0:T(8,128)}) fusion(f32[2,256]{1,0:T(2,128)S(1)} %mul.31, f32[16,128]{1,0:T(8,128)S(1)} %fusion.9), kind=kLoop, calls=%fused_computation | loop fusion | flops 1048576 | bytes 8398848 | tf_op jit(solution)/shard_map/sin | solution.py:541
  45.9 31.7 %all-to-all-done.re.im = bf16[128,8,16,128]{3,2,1,0:T(8,128)(2,1)} async-done(((bf16[128,8,16,128]{3,2,1,0:T(8,128)(2,1)}), bf16[128,8,16,128]{3,2,1,0:T(8,128)(2,1)}, u32[]{:S(2)}, u32[]{:S(2)}) %all-to-all-start) | async-done | bytes 4194336 | tf_op jit(solution)/shard_map/all_to_all | solution.py:572
  77.6 14.6 %azimuth_picture.1.mag = bf16[128,4,16,128]{3,2,1,0:T(8,128)(2,1)} custom-call(bf16[128,8,16,128]{3,2,1,0:T(8,128)(2,1)} %all-to-all-done.re.im, bf16[128,8,16,128]{3,2,1,0:T(8,128)(2,1)} %all-to-all-done.re.im, f32[2,16,128,256]{3,2,1,0:T(8,128)} %get-tuple-element.9.cosine_far, f32[2,16,128,256]{3,2,1,0:T(8,128)} %get-tuple-element.8.sine_far, ...), custom_call_target="tpu_custom_call" | custom-call | tf_op jit(solution)/shard_map/azimuth_picture/pallas_call | solution.py:342
  92.1 0.0 copy-start.5
  92.2 0.0 copy-start.8
  92.2 5.7 %all-to-all-start.1 = ((bf16[128,4,16,128]{3,2,1,0:T(8,128)(2,1)}), bf16[128,4,16,128]{3,2,1,0:T(8,128)(2,1)S(1)}, u32[]{:S(2)}, u32[]{:S(2)}) async-start(bf16[128,4,16,128]{3,2,1,0:T(8,128)(2,1)} %azimuth_picture.1.mag), calls=%async_computation.1 | async-start | bytes 4194304 | tf_op jit(solution)/shard_map/all_to_all | solution.py:578
  97.9 0.0 copy-done.5
  97.9 0.1 slice.19
  98.0 0.5 slice.18
  98.5 0.0 copy-done.8
  98.5 0.1 reshape.154
  98.6 0.1 copy.18
  98.7 0.1 copy.19
  98.8 0.4 reverse.2
  99.2 0.1 slice.24
  99.3 0.8 fusion.1
  100.1 0.2 reshape.155
  100.3 0.2 copy.20
  100.4 1.3 broadcast_in_dim.61.weights
  101.8 0.0 copy-start
  101.8 0.0 copy-start.1
  101.8 0.0 copy-start.2
  101.8 0.0 copy-start.3
  101.8 0.0 copy-start.4
  101.8 17.0 %azimuth_edges.1 = f32[2048,512]{1,0:T(8,128)} custom-call(bf16[128,4,16,128]{3,2,1,0:T(8,128)(2,1)} %azimuth_picture.1.mag, f32[16,128,128]{2,1,0:T(8,128)} %broadcast_in_dim.61.weights, bf16[256,256]{1,0:T(8,128)(2,1)} %constant.84.clone.full, bf16[256,256]{1,0:T(8,128)(2,1)} %constant.85.clone.back, ...), custom_call_target="tpu_custom_call" | custom-call | tf_op jit(solution)/shard_map/azimuth_edges/pallas_call | solution.py:414
  118.8 8.8 %all-to-all-done.1.mag = bf16[128,4,16,128]{3,2,1,0:T(8,128)(2,1)S(1)} async-done(((bf16[128,4,16,128]{3,2,1,0:T(8,128)(2,1)}), bf16[128,4,16,128]{3,2,1,0:T(8,128)(2,1)S(1)}, u32[]{:S(2)}, u32[]{:S(2)}) %all-to-all-start.1) | async-done | bytes 2097184 | tf_op jit(solution)/shard_map/all_to_all | solution.py:578
  127.6 0.0 copy-done
  127.6 0.0 copy-done.1
  127.6 0.0 copy-done.2
  127.6 0.0 copy-done.3
  127.7 0.0 copy-done.4
  127.7 7.1 %range_concentrate.1 = f32[16,65536]{1,0:T(8,128)} custom-call(bf16[128,4,16,128]{3,2,1,0:T(8,128)(2,1)S(1)} %all-to-all-done.1.mag, f32[144,256]{1,0:T(8,128)S(1)} %bitcast.16, bf16[256,256]{1,0:T(8,128)(2,1)S(1)} %copy-done.3, bf16[2,256,256]{2,1,0:T(8,128)(2,1)S(1)} %copy-done.1, bf16[2,256,256]{2,1,0:T(8,128)(2,1)S(1)} %copy-done.2, ...), custom_call_target="tpu_custom_call" | custom-call | tf_op jit(solution)/shard_map/range_concentrate/pallas_call | solution.py:505
  (10 shorter events, 0.1 us)
Async XLA Ops:
  14.4 11.7 %copy-start.9 = (f32[512]{0:T(512)S(1)}, f32[512]{0:T(512)}, u32[]{:S(2)}) copy-start(f32[512]{0:T(512)} %param.18) | copy-start | bytes 6148
  14.4 12.0 %copy-start.6 = (bf16[16,32,256]{2,1,0:T(8,128)(2,1)S(1)}, bf16[16,32,256]{2,1,0:T(8,128)(2,1)}, u32[]{:S(2)}) copy-start(bf16[16,32,256]{2,1,0:T(8,128)(2,1)} %constant.82.clone) | copy-start | bytes 786436
  14.4 12.0 %copy-start.7 = (bf16[16,32,256]{2,1,0:T(8,128)(2,1)S(1)}, bf16[16,32,256]{2,1,0:T(8,128)(2,1)}, u32[]{:S(2)}) copy-start(bf16[16,32,256]{2,1,0:T(8,128)(2,1)} %constant.83.clone) | copy-start | bytes 786436
  14.4 63.2 %all-to-all-start = ((bf16[128,8,16,128]{3,2,1,0:T(8,128)(2,1)}), bf16[128,8,16,128]{3,2,1,0:T(8,128)(2,1)}, u32[]{:S(2)}, u32[]{:S(2)}) async-start(bf16[128,8,16,128]{3,2,1,0:T(8,128)(2,1)} %range_compress.1), calls=%async_computation | async-start | bytes 8388608 | tf_op jit(solution)/shard_map/all_to_all | solution.py:572
  92.1 5.7 %copy-start.5 = (f32[65536]{0:T(1024)S(1)}, f32[65536]{0:T(1024)}, u32[]{:S(2)}) copy-start(f32[65536]{0:T(1024)} %param.20) | copy-start | bytes 786436
  92.2 6.4 %copy-start.8 = (f32[2048]{0:T(1024)S(1)}, f32[2048]{0:T(1024)}, u32[]{:S(2)}) copy-start(f32[2048]{0:T(1024)} %param.19) | copy-start | bytes 24580
  92.2 35.5 %all-to-all-start.1 = ((bf16[128,4,16,128]{3,2,1,0:T(8,128)(2,1)}), bf16[128,4,16,128]{3,2,1,0:T(8,128)(2,1)S(1)}, u32[]{:S(2)}, u32[]{:S(2)}) async-start(bf16[128,4,16,128]{3,2,1,0:T(8,128)(2,1)} %azimuth_picture.1.mag), calls=%async_computation.1 | async-start | bytes 4194304 | tf_op jit(solution)/shard_map/all_to_all | solution.py:578
  101.8 25.9 %copy-start = (f32[2,256,256]{2,1,0:T(8,128)S(1)}, f32[2,256,256]{2,1,0:T(8,128)}, u32[]{:S(2)}) copy-start(f32[2,256,256]{2,1,0:T(8,128)} %constant.77.clone.turns) | copy-start | bytes 1572868
  101.8 25.9 %copy-start.1 = (bf16[2,256,256]{2,1,0:T(8,128)(2,1)S(1)}, bf16[2,256,256]{2,1,0:T(8,128)(2,1)}, u32[]{:S(2)}) copy-start(bf16[2,256,256]{2,1,0:T(8,128)(2,1)} %constant.79.clone.second) | copy-start | bytes 786436
  101.8 25.9 %copy-start.2 = (bf16[2,256,256]{2,1,0:T(8,128)(2,1)S(1)}, bf16[2,256,256]{2,1,0:T(8,128)(2,1)}, u32[]{:S(2)}) copy-start(bf16[2,256,256]{2,1,0:T(8,128)(2,1)} %constant.80.clone.third) | copy-start | bytes 786436
  101.8 25.9 %copy-start.3 = (bf16[256,256]{1,0:T(8,128)(2,1)S(1)}, bf16[256,256]{1,0:T(8,128)(2,1)}, u32[]{:S(2)}) copy-start(bf16[256,256]{1,0:T(8,128)(2,1)} %constant.86.clone.first) | copy-start | bytes 393220
  101.8 25.9 %copy-start.4 = (bf16[256,256]{1,0:T(8,128)(2,1)S(1)}, bf16[256,256]{1,0:T(8,128)(2,1)}, u32[]{:S(2)}) copy-start(bf16[256,256]{1,0:T(8,128)(2,1)} %constant.87.clone.last) | copy-start | bytes 393220

commit v3 on v2

--- a/solution.py
+++ b/solution.py
@@ -34,6 +34,10 @@
     return np.block([[matrix.real, matrix.imag], [-matrix.imag, matrix.real]])
 
 
+def paired(matrix):
+    return matrix.reshape(2, 16, 8, -1).transpose(1, 0, 2, 3).reshape(256, -1)
+
+
 def low(table):
     return np.asarray(table, np.float32).astype(LOW)
 
@@ -43,15 +47,15 @@
     j = np.arange(128)[None, :]
     even = roots(2 * j * k, 256) / 16.0
     odd = roots((2 * j + 1) * k, 256) / 16.0
-    first = np.stack([left_form(even.conj()), left_form(odd.conj())])
+    first = np.stack([paired(left_form(even.conj())), paired(left_form(odd.conj()))])
     second = np.stack([right_form(even.conj()), right_form(odd.conj())])
     third = np.stack([right_form(even.T), right_form(odd.T)])
     fourth = np.stack([left_form(even.T), left_form(odd.T)])
     return tuple(low(t) for t in (first, second, third, fourth))
 
 
-def range_turns(rows):
-    table = roots(np.arange(rows)[:, None] * np.arange(256)[None, :], BINS)
+def range_turns():
+    table = paired(roots(np.arange(256)[:, None] * np.arange(256)[None, :], BINS))
     return np.stack([table.real, table.imag]).astype(np.float32)
 
 
@@ -62,13 +66,13 @@
     mirror = np.cos(math.pi * n) / 16.0
     first = np.concatenate([base.real, mirror, -base.imag[1:]], 0)
     last = np.concatenate([base.real.T, mirror.T, -base.imag[1:].T], 1)
-    return low(first), low(last)
+    return low(paired(first)), low(last)
 
 
 def azimuth_tables():
     s = np.arange(128)
     outer = roots(-s[:, None] * s[None, :], 128) / math.sqrt(128.0)
-    full = left_form(outer).reshape(2, 16, 8, 256).transpose(1, 0, 2, 3).reshape(256, 256)
+    full = paired(left_form(outer))
     group = np.arange(16)[:, None, None, None]
     eight = np.arange(8)[None, None, None, :]
     fb = np.arange(16)[None, :, None, None]
@@ -77,7 +81,7 @@
     pair = np.stack([np.stack([inner.real, -inner.imag], 3), np.stack([inner.imag, inner.real], 3)], 2)
     forward = pair.reshape(16, 32, 256)
     backward = pair.transpose(0, 3, 4, 1, 2, 5).reshape(16, 32, 256)
-    return low(full), low(full.T), low(forward), low(backward)
+    return low(full), low(paired(full.T)), low(full.T[:128]), low(forward), low(backward)
 
 
 def dot(a, b):
@@ -97,35 +101,49 @@
 
 
 def together(jobs):
-    while jobs:
-        jobs = [job for job in jobs if next(job, None) is not None]
-
-
-def forward_spectrum(parts, turns, second):
-    sums, gaps = [], []
-    for re, im, rows in parts:
-        c, s = turns[0, rows, :], turns[1, rows, :]
-        tr = re * c + im * s
-        ti = im * c - re * s
-        sums.append(beside(tr[:, :128] + tr[:, 128:], ti[:, :128] + ti[:, 128:]).astype(LOW))
-        gaps.append(beside(tr[:, :128] - tr[:, 128:], ti[:, :128] - ti[:, 128:]).astype(LOW))
-    return (
-        dot(jnp.concatenate(sums, 0), second[0]),
-        dot(jnp.concatenate(gaps, 0), second[1]),
-    )
-
-
-def back_section(even, odd, turns, third):
-    even = dot(even, third[0])
-    odd = dot(odd, third[1])
-    rows = even.shape[0]
-    halves = []
-    for h, b in enumerate((even + odd, even - odd)):
-        c = turns[0, :rows, h * 128 : h * 128 + 128]
-        s = turns[1, :rows, h * 128 : h * 128 + 128]
-        re, im = b[:, :128], b[:, 128:]
-        halves.append((re * c - im * s, re * s + im * c))
-    return halves
+    asked = [next(job) for job in jobs]
+    while asked:
+        sent = [None] * len(jobs)
+        if asked[0] is not None:
+            rows = asked[0][0].shape[0]
+            results = []
+            for e in range(2):
+                lhs = jnp.concatenate([ask[e] for ask in asked], 0)
+                results.append(dot(lhs, asked[0][2][e]))
+            sent = [[r[n * rows : n * rows + rows] for r in results] for n in range(len(jobs))]
+        nexts = []
+        for job, value in zip(jobs, sent):
+            try:
+                nexts.append(job.send(value))
+            except StopIteration:
+                pass
+        asked = nexts
+
+
+def groups(value):
+    return value.reshape(-1, 2, 8, value.shape[-1])
+
+
+def halves(value):
+    return value[..., :128], value[..., 128:]
+
+
+def flat(value):
+    return value.reshape(-1, value.shape[-1])
+
+
+def turned_back(re, im, c, s):
+    return re * c + im * s, im * c - re * s
+
+
+def turned_on(re, im, c, s):
+    return re * c - im * s, re * s + im * c
+
+
+def sum_and_gap(re, im):
+    (r0, r1), (i0, i1) = halves(re), halves(im)
+    join = lambda a, b: jnp.concatenate([a, b], -1)
+    return join(r0 + r1, i0 + i1), join(r0 - r1, i0 - i1)
 
 
 def sine_cosine(x):
@@ -150,8 +168,10 @@
             for h in range(2):
                 part = angles[pl.ds(2 * e + h, 128, stride=4), :]
                 sine, cosine = sine_cosine(part.T)
-                phase[0, h * 128 : h * 128 + 128, e * 128 : e * 128 + 128] = cosine
-                phase[1, h * 128 : h * 128 + 128, e * 128 : e * 128 + 128] = sine
+                for t in range(16):
+                    rows = slice(t * 16 + h * 8, t * 16 + h * 8 + 8)
+                    phase[0, rows, e * 128 : e * 128 + 128] = cosine[t * 8 : t * 8 + 8]
+                    phase[1, rows, e * 128 : e * 128 + 128] = sine[t * 8 : t * 8 + 8]
 
     @pl.when(step < FILLS)
     def _():
@@ -194,23 +214,34 @@
 
             return above(half(0), half(1)).astype(LOW)
 
-        even = dot(first[0], load(0))
-        odd = dot(first[1], load(1))
-        yield 1
-        lo, hi = even + odd, even - odd
-        parts = [(v[:128], v[128:], slice(r, r + 128)) for v, r in ((lo, 0), (hi, 128))]
+        even = groups(dot(first[0], load(0)))
+        odd = groups(dot(first[1], load(1)))
+        yield
+        c, s = groups(turns[0]), groups(turns[1])
+        parts = []
+        for h, v in enumerate((even + odd, even - odd)):
+            parts.append(sum_and_gap(*turned_back(v[:, 0], v[:, 1], c[:, h], s[:, h])))
+        zs = [flat(jnp.stack([parts[0][e], parts[1][e]], 1)).astype(LOW) for e in range(2)]
+        zs = yield (zs[0], zs[1], second)
         turned = []
-        for e, z in enumerate(forward_spectrum(parts, turns, second)):
-            c = phase[0, :, e * 128 : e * 128 + 128]
-            s = phase[1, :, e * 128 : e * 128 + 128]
-            re, im = z[:, :128], z[:, 128:]
-            turned.append(beside(re * c - im * s, re * s + im * c).astype(LOW))
-        yield 1
-        (r0, i0), (r1, i1) = back_section(turned[0], turned[1], turns, third)
-        re, im = beside(r0, r1), beside(i0, i1)
-        sums = above(re[:128] + re[128:], im[:128] + im[128:]).astype(LOW)
-        gaps = above(re[:128] - re[128:], im[:128] - im[128:]).astype(LOW)
-        yield 1
+        for e in range(2):
+            re, im = halves(zs[e])
+            at = slice(e * 128, e * 128 + 128)
+            turned.append(beside(*turned_on(re, im, phase[0, :, at], phase[1, :, at])).astype(LOW))
+        even, odd = yield (turned[0], turned[1], third)
+        even, odd = groups(even), groups(odd)
+        sums, gaps = [], []
+        for h, b in enumerate((even + odd, even - odd)):
+            at = slice(h * 128, h * 128 + 128)
+            re, im = halves(b)
+            re, im = turned_on(re, im, groups(turns[0])[..., at], groups(turns[1])[..., at])
+            sums.append((flat(re[:, 0] + re[:, 1]), flat(im[:, 0] + im[:, 1])))
+            gaps.append((flat(re[:, 0] - re[:, 1]), flat(im[:, 0] - im[:, 1])))
+        sums, gaps = (
+            above(beside(v[0][0], v[1][0]), beside(v[0][1], v[1][1])).astype(LOW)
+            for v in (sums, gaps)
+        )
+        yield
         for o, c in enumerate((dot(fourth[0], sums), dot(fourth[1], gaps))):
             for part in range(2):
                 for h in range(2):
@@ -247,16 +278,16 @@
     )(raw, angles, *tables, turns)
 
 
-def spread_rows(source, xs):
+def spread_rows(*pairs):
     def move(n, _):
-        for u in range(8):
-            at = n * 8 + u
-            for h in range(2):
-                v = source[at, h].astype(F32)
-                xs[h, pl.ds(at * PITCH, ROWS), :] = v
-        return 0
-
-    lax.fori_loop(0, 16, move, 0)
+        for u in range(16 // len(pairs)):
+            at = n * (16 // len(pairs)) + u
+            for source, xs in pairs:
+                for h in range(2):
+                    xs[h, pl.ds(at * PITCH, ROWS), :] = source[at, h].astype(F32)
+        return 0
+
+    lax.fori_loop(0, OWNERS * len(pairs) // 16, move, 0)
 
 
 def pulse_rows(xs, p):
@@ -283,15 +314,14 @@
         for table in tables:
             table.start()
 
-    spread_rows(re, xr)
-    spread_rows(im, xi)
+    spread_rows((re, xr), (im, xi))
 
     def outer(p, _):
         x = above(pulse_rows(xr, p), pulse_rows(xi, p)).astype(LOW)
         ys[p] = dot(full[...], x).astype(LOW)
         return 0
 
-    lax.fori_loop(0, 16, outer, 0, unroll=8)
+    lax.fori_loop(0, 16, outer, 0, unroll=16)
 
     @pl.when(step == 0)
     def _():
@@ -303,22 +333,27 @@
         for table in tables[4:]:
             table.wait()
 
-    def inner(g, _):
-        rows = pl.ds(pl.multiple_of(g * 16, 16), 16)
-        y = dot(forward[g], ys[:, rows, :].reshape(256, 256)).reshape(16, 2, 8, 256)
-        c = cosine[step, g].reshape(16, 8, 256)
-        s = sine[step, g].reshape(16, 8, 256)
-        zr = y[:, 0] * c - y[:, 1] * s
-        zi = y[:, 0] * s + y[:, 1] * c
-        z = jnp.stack([zr, zi], 1).reshape(256, 256).astype(LOW)
-        vs[:, rows, :] = dot(backward[g], z).astype(LOW).reshape(16, 16, 256)
-        return 0
-
-    lax.fori_loop(0, 16, inner, 0, unroll=4)
+    def inner(n, _):
+        at = [n * 8 + u for u in range(8)]
+        rows = [pl.ds(pl.multiple_of(g * 16, 16), 16) for g in at]
+        ahead = [dot(forward[g], ys[:, r, :].reshape(256, 256)) for g, r in zip(at, rows)]
+        turned = []
+        for g, y in zip(at, ahead):
+            y = groups(y)
+            c = cosine[step, g].reshape(16, 8, 256)
+            s = sine[step, g].reshape(16, 8, 256)
+            z = jnp.stack(turned_on(y[:, 0], y[:, 1], c, s), 1)
+            turned.append(flat(z).astype(LOW))
+        for g, r, z in zip(at, rows, turned):
+            vs[:, r, :] = dot(backward[g], z).astype(LOW).reshape(16, 16, 256)
+        return 0
+
+    lax.fori_loop(0, 2, inner, 0)
 
     def last(p, _):
         x = dot(back[...], vs[p])
-        a, b = x[:128], x[128:]
+        x = groups(x)
+        a, b = flat(x[:, 0]), flat(x[:, 1])
         m = a * a + b * b
         m = m * lax.rsqrt(jnp.maximum(m, SMALLEST))
         at = pl.ds(p, 128, stride=PITCH)
@@ -326,7 +361,7 @@
         ms[1, at, :] = m[:, 128:]
         return 0
 
-    lax.fori_loop(0, 16, last, 0, unroll=8)
+    lax.fori_loop(0, 16, last, 0, unroll=16)
 
     def gather(n, _):
         for u in range(8):
@@ -371,7 +406,7 @@
 
 
 def edge_kernel(mag, weights, full, back, forward, backward, out, xs, ys, vs, ms):
-    spread_rows(mag, xs)
+    spread_rows((mag, xs))
 
     def outer(p, _):
         ys[p] = dot(full[:, :128], pulse_rows(xs, p).astype(LOW)).astype(LOW)
@@ -391,7 +426,7 @@
     lax.fori_loop(0, 16, inner, 0, unroll=2)
 
     def last(p, _):
-        x = dot(back[:128, :], vs[p])
+        x = dot(back[...], vs[p])
         at = pl.ds(p, 128, stride=PITCH)
         ms[0, at, :] = x[:, :128]
         ms[1, at, :] = x[:, 128:]
@@ -418,7 +453,7 @@
             pl.BlockSpec((OWNERS, 2, ROWS, 128), lambda i: (0, i, 0, 0)),
             whole((16, 128, 128)),
             whole((256, 256)),
-            whole((256, 256)),
+            whole((128, 256)),
             whole((16, 256, 256)),
             whole((16, 256, 256)),
         ],
@@ -467,27 +502,39 @@
 
 
 def concentrate_pulses(weights, first, second, third, last, turns, xs, os):
-    top = lax.broadcasted_iota(jnp.int32, (128, 256), 0) == 0
+    top = lax.broadcasted_iota(jnp.int32, (8, 256), 0) == 0
 
     def one(p):
         at = pl.ds(p, 128, stride=PITCH)
         x = above(beside(xs[0, at, :], xs[1, at, :]), beside(xs[2, at, :], xs[3, at, :]))
-        y = dot(first[...], x.astype(LOW))
-        yield 1
-        re, im = y[:128], y[128:]
-        mirror = jnp.where(top[:16], im[:16], 0.0)
-        im = jnp.where(top, 0.0, im)
-        parts = [(re, im, slice(0, 128)), (mirror, jnp.zeros_like(mirror), slice(128, 144))]
+        y = groups(dot(first[...], x.astype(LOW)))
+        yield
+        re, im = flat(y[:, 0]), flat(y[:, 1])
+        mirror = jnp.where(top, im[:8], 0.0)
+        im = above(jnp.where(top, 0.0, im[:8]), im[8:])
+        c, s = groups(turns[0]), groups(turns[1])
+        body = sum_and_gap(*turned_back(re, im, flat(c[:, 0]), flat(s[:, 0])))
+        tail = sum_and_gap(mirror * c[0, 1], -mirror * s[0, 1])
+        rows = [jnp.concatenate([body[e], tail[e], jnp.zeros_like(tail[e])], 0) for e in range(2)]
+        zs = yield (rows[0].astype(LOW), rows[1].astype(LOW), second)
         jumped = []
-        for e, z in enumerate(forward_spectrum(parts, turns, second)):
+        for e in range(2):
+            re, im = halves(zs[e])
             w = weights[:, e * 128 : e * 128 + 128]
-            jumped.append(beside(-z[:, 128:] * w, z[:, :128] * w).astype(LOW))
-        yield 1
-        (r0, i0), (r1, i1) = back_section(jumped[0], jumped[1], turns, third)
-        re, im = beside(r0, r1), beside(i0, i1)
-        im = above(jnp.where(top[:8], re[128:136], im[:8]), im[8:128])
-        yield 1
-        e = dot(last[...], above(re[:128], im).astype(LOW))
+            jumped.append(beside(-im * w, re * w).astype(LOW))
+        even, odd = yield (jumped[0], jumped[1], third)
+        res, ims = [], []
+        for h, b in enumerate((even + odd, even - odd)):
+            at = slice(h * 128, h * 128 + 128)
+            re, im = halves(b)
+            c = groups(turns[0])[..., at]
+            s = groups(turns[1])[..., at]
+            r, i = turned_on(re[:128], im[:128], flat(c[:, 0]), flat(s[:, 0]))
+            mirror = re[128:136] * c[0, 1] - im[128:136] * s[0, 1]
+            res.append(r)
+            ims.append(above(jnp.where(top[:, :128], mirror, i[:8]), i[8:]))
+        yield
+        e = dot(last[...], above(beside(*res), beside(*ims)).astype(LOW))
         for o in range(2):
             for h in range(2):
                 os[h, pl.ds(o * PITCH + p, 128, stride=2 * PITCH), :] = e[
@@ -566,17 +613,19 @@
 
 def on_device(raw_pulses, range_phase, azimuth_rate, conc_azimuth, conc_range):
     first, second, third, fourth = range_tables()
-    turns = jnp.asarray(range_turns(256))
+    turns = jnp.asarray(range_turns())
     angles = range_phase.reshape(512, 128)
     blocks = range_compress(raw_pulses, angles, (first, second, third, fourth), turns)
     received = lax.all_to_all(blocks, AXES, split_axis=0, concat_axis=0, tiled=True)
-    full, back, forward, backward = azimuth_tables()
+    full, back, real_back, forward, backward = azimuth_tables()
     forward, backward, _ = lax.optimization_barrier((forward, backward, conc_azimuth))
     forward, backward = expand(forward), expand(backward)
     cosine, sine = azimuth_phase(azimuth_rate)
     mag = azimuth_picture(received, cosine, sine, full, back, forward, backward)
     shared = lax.all_to_all(mag, AXES, split_axis=0, concat_axis=0, tiled=True)
-    edge_azimuth = azimuth_edges(mag, azimuth_weights(conc_azimuth), full, back, forward, backward)
+    edge_azimuth = azimuth_edges(
+        mag, azimuth_weights(conc_azimuth), full, real_back, forward, backward
+    )
     real_first, real_last = real_range_tables()
     edge_range = range_concentrate(
         shared, range_weights(conc_range), real_first, second, third, real_last, turns

time: 135 us -> 132 us (0.978)
  Pallas kernels: 52.4 us -> 48.8 us
    pallas_call x1, Pallas kernels: 14.6 us -> 12 us  [azimuth_picture(): pl.pallas_call(picture_kernel, grid=(2,), in_specs=[pl.BlockSpec((OWNERS,...]
  transfers between devices with their start and end apart: 2 -> 2, of which waited for: 2 -> 2; matrix products, arithmetic and copies ran while one was open for 17% -> 18% of each run, Pallas kernels for 13% -> 13%
where the time goes in v3:
time: 132 us; the launch traced here: 131 us
  Pallas kernels  48.8 us (37%)
  waiting for transfers between devices  40.6 us (31%)
  other arithmetic  20.3 us (15%)
  starting transfers between devices  17.4 us (13%)
  local copies, waits for them, and re-layouts  3.3 us (2%)
    all_to_all x1, waiting for transfers between devices, on_device(): lax.all_to_all(blocks, AXES, split_axis=0, concat_axis=0, tiled=True)  31.7 us
    pallas_call x1, Pallas kernels, azimuth_edges(): pl.pallas_call(edge_kernel, grid=(2,), in_specs=[pl.BlockSpec((OWNERS, 2,...  16.9 us
    sin x1, other arithmetic, azimuth_phase(): return (jnp.cos(angles), jnp.sin(angles))  16.9 us
    pallas_call x1, Pallas kernels, range_compress(): pl.pallas_call(compress_kernel, grid=(2 * FILLS,), in_specs=[pl.BlockSpec...  13.2 us
    pallas_call x1, Pallas kernels, azimuth_picture(): pl.pallas_call(picture_kernel, grid=(2,), in_specs=[pl.BlockSpec((OWNERS,...  12 us
    all_to_all x1, starting transfers between devices, on_device(): lax.all_to_all(blocks, AXES, split_axis=0, concat_axis=0, tiled=True)  11.7 us
    all_to_all x1, waiting for transfers between devices, on_device(): shared = lax.all_to_all(mag, AXES, split_axis=0, concat_axis=0, tiled=True)  8.9 us
    pallas_call x1, Pallas kernels, range_concentrate(): pl.pallas_call(concentrate_kernel, grid=(2 + FILLS,), in_specs=[pl.BlockS...  6.74 us
  transfers between devices with their start and end apart: 2, of which 2 were waited for; matrix products, arithmetic and copies ran while one was open for 18% of the time, Pallas kernels for 13%

profile of v3, /device:TPU:0, one launch (start us, length us, event | category | flops | bytes accessed | tf_op | source)
XLA Modules:
  0.0 131.2 jit_solution(16232989351918942512)
XLA Ops:
  0.6 13.2 %range_compress.1 = bf16[128,8,16,128]{3,2,1,0:T(8,128)(2,1)} custom-call(bf16[2,16,65536]{2,1,0:T(8,128)(2,1)} %raw.1, f32[512,128]{1,0:T(8,128)} %bitcast.21, bf16[2,256,256]{2,1,0:T(8,128)(2,1)} %constant.80.clone.first, bf16[2,256,256]{2,1,0:T(8,128)(2,1)} %constant.81.clone.second, bf16[2,256,256]{2,1,0:T(8,128)(2,1)} %constant.82.clone.third, ...), custom_call_target="tpu_custom_call" | custom-call | tf_op jit(solution)/shard_map/range_compress/pallas_call | solution.py:260
  13.8 0.0 copy-start.9
  13.8 0.0 copy-start.6
  13.8 0.0 copy-start.7
  13.8 11.7 %all-to-all-start = ((bf16[128,8,16,128]{3,2,1,0:T(8,128)(2,1)}), bf16[128,8,16,128]{3,2,1,0:T(8,128)(2,1)}, u32[]{:S(2)}, u32[]{:S(2)}) async-start(bf16[128,8,16,128]{3,2,1,0:T(8,128)(2,1)} %range_compress.1), calls=%async_computation | async-start | bytes 8388608 | tf_op jit(solution)/shard_map/all_to_all | solution.py:619
  25.5 0.0 copy-done.9
  25.6 0.1 reshape.152
  25.7 0.1 iota.64
  25.8 0.0 copy-done.6
  25.9 0.0 copy-done.7
  25.9 2.6 %bitcast_select_fusion = (bf16[16,256,256]{2,1,0:T(8,128)(2,1)}, bf16[16,256,256]{2,1,0:T(8,128)(2,1)}) fusion(pred[256,256]{1,0:T(8,128)(4,1)S(1)} %broadcast_bitcast_fusion, bf16[16,32,256]{2,1,0:T(8,128)(2,1)S(1)} %copy-done.7, bf16[16,32,256]{2,1,0:T(8,128)(2,1)S(1)} %copy-done.6), kind=kLoop, calls=%fused_computation.2 | loop fusion | flops 2097152 | bytes 4784128 | tf_op jit(solution)/shard_map/jit(_where)/select_n | solution.py:610
  28.4 16.9 %multiply_sine_fusion = (f32[2,16,128,256]{3,2,1,0:T(8,128)}, f32[2,16,128,256]{3,2,1,0:T(8,128)}) fusion(f32[2,256]{1,0:T(2,128)S(1)} %mul.31, f32[16,128]{1,0:T(8,128)S(1)} %fusion.9), kind=kLoop, calls=%fused_computation | loop fusion | flops 1048576 | bytes 8398848 | tf_op jit(solution)/shard_map/sin | solution.py:588
  45.3 31.7 %all-to-all-done.re.im = bf16[128,8,16,128]{3,2,1,0:T(8,128)(2,1)} async-done(((bf16[128,8,16,128]{3,2,1,0:T(8,128)(2,1)}), bf16[128,8,16,128]{3,2,1,0:T(8,128)(2,1)}, u32[]{:S(2)}, u32[]{:S(2)}) %all-to-all-start) | async-done | bytes 4194336 | tf_op jit(solution)/shard_map/all_to_all | solution.py:619
  77.0 12.0 %azimuth_picture.1.mag = bf16[128,4,16,128]{3,2,1,0:T(8,128)(2,1)} custom-call(bf16[128,8,16,128]{3,2,1,0:T(8,128)(2,1)} %all-to-all-done.re.im, bf16[128,8,16,128]{3,2,1,0:T(8,128)(2,1)} %all-to-all-done.re.im, f32[2,16,128,256]{3,2,1,0:T(8,128)} %get-tuple-element.9.cosine_far, f32[2,16,128,256]{3,2,1,0:T(8,128)} %get-tuple-element.8.sine_far, ...), custom_call_target="tpu_custom_call" | custom-call | tf_op jit(solution)/shard_map/azimuth_picture/pallas_call | solution.py:377
  89.0 0.0 copy-start.5
  89.0 0.0 copy-start.8
  89.0 5.7 %all-to-all-start.1 = ((bf16[128,4,16,128]{3,2,1,0:T(8,128)(2,1)}), bf16[128,4,16,128]{3,2,1,0:T(8,128)(2,1)S(1)}, u32[]{:S(2)}, u32[]{:S(2)}) async-start(bf16[128,4,16,128]{3,2,1,0:T(8,128)(2,1)} %azimuth_picture.1.mag), calls=%async_computation.1 | async-start | bytes 4194304 | tf_op jit(solution)/shard_map/all_to_all | solution.py:625
  94.7 0.0 copy-done.5
  94.7 0.1 slice.19
  94.8 0.5 slice.18
  95.4 0.0 copy-done.8
  95.4 0.1 reshape.154
  95.5 0.1 copy.19
  95.6 0.1 copy.20
  95.6 0.4 reverse.2
  96.0 0.1 slice.24
  96.1 0.8 fusion.1
  96.9 0.2 reshape.155
  97.1 0.2 copy.21
  97.3 1.3 broadcast_in_dim.61.weights
  98.6 0.0 copy-start
  98.6 0.0 copy-start.1
  98.6 0.0 copy-start.2
  98.6 0.0 copy-start.3
  98.6 0.0 copy-start.4
  98.6 16.9 %azimuth_edges.1 = f32[2048,512]{1,0:T(8,128)} custom-call(bf16[128,4,16,128]{3,2,1,0:T(8,128)(2,1)} %azimuth_picture.1.mag, f32[16,128,128]{2,1,0:T(8,128)} %broadcast_in_dim.61.weights, bf16[256,256]{1,0:T(8,128)(2,1)} %constant.86.clone.full, bf16[128,256]{1,0:T(8,128)(2,1)} %constant.88.clone.back, ...), custom_call_target="tpu_custom_call" | custom-call | tf_op jit(solution)/shard_map/azimuth_edges/pallas_call | solution.py:449
  115.6 8.9 %all-to-all-done.1.mag = bf16[128,4,16,128]{3,2,1,0:T(8,128)(2,1)S(1)} async-done(((bf16[128,4,16,128]{3,2,1,0:T(8,128)(2,1)}), bf16[128,4,16,128]{3,2,1,0:T(8,128)(2,1)S(1)}, u32[]{:S(2)}, u32[]{:S(2)}) %all-to-all-start.1) | async-done | bytes 2097184 | tf_op jit(solution)/shard_map/all_to_all | solution.py:625
  124.5 0.0 copy-done
  124.5 0.0 copy-done.1
  124.5 0.0 copy-done.2
  124.5 0.0 copy-done.3
  124.5 0.0 copy-done.4
  124.5 6.7 %range_concentrate.1 = f32[16,65536]{1,0:T(8,128)} custom-call(bf16[128,4,16,128]{3,2,1,0:T(8,128)(2,1)S(1)} %all-to-all-done.1.mag, f32[144,256]{1,0:T(8,128)S(1)} %bitcast.16, bf16[256,256]{1,0:T(8,128)(2,1)S(1)} %copy-done.3, bf16[2,256,256]{2,1,0:T(8,128)(2,1)S(1)} %copy-done.1, bf16[2,256,256]{2,1,0:T(8,128)(2,1)S(1)} %copy-done.2, ...), custom_call_target="tpu_custom_call" | custom-call | tf_op jit(solution)/shard_map/range_concentrate/pallas_call | solution.py:552
  (10 shorter events, 0.1 us)
Async XLA Ops:
  13.8 11.7 %copy-start.9 = (f32[512]{0:T(512)S(1)}, f32[512]{0:T(512)}, u32[]{:S(2)}) copy-start(f32[512]{0:T(512)} %param.19) | copy-start | bytes 6148
  13.8 12.0 %copy-start.6 = (bf16[16,32,256]{2,1,0:T(8,128)(2,1)S(1)}, bf16[16,32,256]{2,1,0:T(8,128)(2,1)}, u32[]{:S(2)}) copy-start(bf16[16,32,256]{2,1,0:T(8,128)(2,1)} %constant.84.clone) | copy-start | bytes 786436
  13.8 12.0 %copy-start.7 = (bf16[16,32,256]{2,1,0:T(8,128)(2,1)S(1)}, bf16[16,32,256]{2,1,0:T(8,128)(2,1)}, u32[]{:S(2)}) copy-start(bf16[16,32,256]{2,1,0:T(8,128)(2,1)} %constant.85.clone) | copy-start | bytes 786436
  13.8 63.2 %all-to-all-start = ((bf16[128,8,16,128]{3,2,1,0:T(8,128)(2,1)}), bf16[128,8,16,128]{3,2,1,0:T(8,128)(2,1)}, u32[]{:S(2)}, u32[]{:S(2)}) async-start(bf16[128,8,16,128]{3,2,1,0:T(8,128)(2,1)} %range_compress.1), calls=%async_computation | async-start | bytes 8388608 | tf_op jit(solution)/shard_map/all_to_all | solution.py:619
  89.0 5.7 %copy-start.5 = (f32[65536]{0:T(1024)S(1)}, f32[65536]{0:T(1024)}, u32[]{:S(2)}) copy-start(f32[65536]{0:T(1024)} %param.21) | copy-start | bytes 786436
  89.0 6.4 %copy-start.8 = (f32[2048]{0:T(1024)S(1)}, f32[2048]{0:T(1024)}, u32[]{:S(2)}) copy-start(f32[2048]{0:T(1024)} %param.20) | copy-start | bytes 24580
  89.0 35.5 %all-to-all-start.1 = ((bf16[128,4,16,128]{3,2,1,0:T(8,128)(2,1)}), bf16[128,4,16,128]{3,2,1,0:T(8,128)(2,1)S(1)}, u32[]{:S(2)}, u32[]{:S(2)}) async-start(bf16[128,4,16,128]{3,2,1,0:T(8,128)(2,1)} %azimuth_picture.1.mag), calls=%async_computation.1 | async-start | bytes 4194304 | tf_op jit(solution)/shard_map/all_to_all | solution.py:625
  98.6 25.9 %copy-start = (f32[2,256,256]{2,1,0:T(8,128)S(1)}, f32[2,256,256]{2,1,0:T(8,128)}, u32[]{:S(2)}) copy-start(f32[2,256,256]{2,1,0:T(8,128)} %constant.79.clone.turns) | copy-start | bytes 1572868
  98.6 25.9 %copy-start.1 = (bf16[2,256,256]{2,1,0:T(8,128)(2,1)S(1)}, bf16[2,256,256]{2,1,0:T(8,128)(2,1)}, u32[]{:S(2)}) copy-start(bf16[2,256,256]{2,1,0:T(8,128)(2,1)} %constant.81.clone.second) | copy-start | bytes 786436
  98.6 25.9 %copy-start.2 = (bf16[2,256,256]{2,1,0:T(8,128)(2,1)S(1)}, bf16[2,256,256]{2,1,0:T(8,128)(2,1)}, u32[]{:S(2)}) copy-start(bf16[2,256,256]{2,1,0:T(8,128)(2,1)} %constant.82.clone.third) | copy-start | bytes 786436
  98.6 25.9 %copy-start.3 = (bf16[256,256]{1,0:T(8,128)(2,1)S(1)}, bf16[256,256]{1,0:T(8,128)(2,1)}, u32[]{:S(2)}) copy-start(bf16[256,256]{1,0:T(8,128)(2,1)} %constant.89.clone.first) | copy-start | bytes 393220
  98.6 25.9 %copy-start.4 = (bf16[256,256]{1,0:T(8,128)(2,1)S(1)}, bf16[256,256]{1,0:T(8,128)(2,1)}, u32[]{:S(2)}) copy-start(bf16[256,256]{1,0:T(8,128)(2,1)} %constant.90.clone.last) | copy-start | bytes 393220

commit v4 on v3

--- a/solution.py
+++ b/solution.py
@@ -13,6 +13,7 @@
 PULSES = 2048
 ROWS = 16
 PITCH = 18
+NARROW = 9
 SMALLEST = float(np.finfo(np.float32).tiny)
 FILLS = 4
 OWNERS = 128
@@ -159,60 +160,53 @@
     return 2.0 * s * c, 1.0 - 2.0 * s * s
 
 
-def compress_kernel(raw, angles, first, second, third, fourth, turns, out, xs, os, phase):
-    step = pl.program_id(0)
-
-    @pl.when(step == 0)
-    def _():
-        for e in range(2):
-            for h in range(2):
-                part = angles[pl.ds(2 * e + h, 128, stride=4), :]
-                sine, cosine = sine_cosine(part.T)
-                for t in range(16):
-                    rows = slice(t * 16 + h * 8, t * 16 + h * 8 + 8)
-                    phase[0, rows, e * 128 : e * 128 + 128] = cosine[t * 8 : t * 8 + 8]
-                    phase[1, rows, e * 128 : e * 128 + 128] = sine[t * 8 : t * 8 + 8]
-
-    @pl.when(step < FILLS)
-    def _():
-        def spread(n, _):
-            for u in range(8):
-                at = n * 8 + u
-                for c in range(2):
-                    v = raw[c, :, pl.ds(pl.multiple_of(at * 256, 256), 256)].astype(F32)
-                    row = (step * (256 // FILLS) + at) * PITCH
-                    xs[c, 0, pl.ds(row, ROWS), :] = v[:, :128]
-                    xs[c, 1, pl.ds(row, ROWS), :] = v[:, 128:]
-            return 0
-
-        lax.fori_loop(0, 32 // FILLS, spread, 0)
-
-    @pl.when(step == FILLS - 1)
-    def _():
-        compress_pulses(first, second, third, fourth, turns, xs, os, phase)
-
-    @pl.when(step >= FILLS)
-    def _():
-        def gather(n, _):
-            for u in range(4):
-                at = n * 4 + u
-                row = ((step - FILLS) * (OWNERS // FILLS) + at) * PITCH
-                for k in range(8):
-                    v = os[k, pl.ds(row, ROWS), :].astype(LOW)
-                    out[at, k] = v
-            return 0
-
-        lax.fori_loop(0, OWNERS // FILLS // 4, gather, 0)
-
-
-def compress_pulses(first, second, third, fourth, turns, xs, os, phase):
-    def one(p):
+def compress_kernel(
+    raw_far, angles_far, first_far, second_far, third_far, fourth_far, turns_far, out_far,
+    raw, angles, first, second, third, fourth, turns, xs, os, phase, packed, arrived, left,
+):
+    here = [
+        (angles_far, angles),
+        (raw_far.at[:, pl.ds(0, 8), :], raw.at[0]),
+        (turns_far, turns),
+        (first_far, first),
+        (second_far, second),
+        (third_far, third),
+        (fourth_far, fourth),
+    ]
+    here.append((raw_far.at[:, pl.ds(8, 8), :], raw.at[1]))
+    here = [pltpu.make_async_copy(a, b, arrived.at[n]) for n, (a, b) in enumerate(here)]
+    for copy in here:
+        copy.start()
+
+    def sending(half, part):
+        some = pl.ds(part * (OWNERS // 2), OWNERS // 2)
+        return pltpu.make_async_copy(
+            packed.at[half, some], out_far.at[some, half], left.at[2 * half + part]
+        )
+
+    def spread(half, n):
+        lane, row = pl.multiple_of(n * 4096, 4096), n * (16 * NARROW)
+        for c in range(2):
+            v = raw[half, c, :, pl.ds(lane, 4096)]
+            for u in range(16):
+                for h in range(2):
+                    at = (2 * u + h) * 128
+                    xs[half, c, h, pl.ds(row + u * NARROW, 8), :] = v[:, at : at + 128].astype(F32)
+
+    def gather(half, n):
+        base, row = n * 8, n * (8 * PITCH)
+        for u in range(8):
+            for k in range(4):
+                v = os[half, k, pl.ds(row + u * PITCH, ROWS), :]
+                packed[half, base + u, k] = v.astype(LOW)
+
+    def one(half, p):
         def load(odd):
-            def half(c):
-                at = pl.ds(odd * PITCH + p, 128, stride=2 * PITCH)
-                return beside(xs[c, 0, at, :], xs[c, 1, at, :])
-
-            return above(half(0), half(1)).astype(LOW)
+            def wide(c):
+                at = pl.ds(odd * NARROW + p, 128, stride=2 * NARROW)
+                return beside(xs[half, c, 0, at, :], xs[half, c, 1, at, :])
+
+            return above(wide(0), wide(1)).astype(LOW)
 
         even = groups(dot(first[0], load(0)))
         odd = groups(dot(first[1], load(1)))
@@ -245,34 +239,82 @@
         for o, c in enumerate((dot(fourth[0], sums), dot(fourth[1], gaps))):
             for part in range(2):
                 for h in range(2):
-                    os[part * 4 + o * 2 + h, pl.ds(p, 128, stride=PITCH), :] = c[
+                    os[half, o * 2 + h, pl.ds(part * 8 + p, 128, stride=PITCH), :] = c[
                         part * 128 : part * 128 + 128, h * 128 : h * 128 + 128
                     ]
 
-    def some(i, _):
-        together([one(4 * i + u) for u in range(4)])
-        return 0
-
-    lax.fori_loop(0, ROWS // 4, some, 0)
+    here[0].wait()
+    for e in range(2):
+        for h in range(2):
+            part = angles[pl.ds(2 * e + h, 128, stride=4), :]
+            sine, cosine = sine_cosine(part.T)
+            for t in range(16):
+                rows = slice(t * 16 + h * 8, t * 16 + h * 8 + 8)
+                phase[0, rows, e * 128 : e * 128 + 128] = cosine[t * 8 : t * 8 + 8]
+                phase[1, rows, e * 128 : e * 128 + 128] = sine[t * 8 : t * 8 + 8]
+
+    def one_half(half, _):
+        @pl.when(half == 0)
+        def _():
+            here[1].wait()
+
+        @pl.when(half == 1)
+        def _():
+            here[7].wait()
+
+        def spread_some(n, _):
+            spread(half, n)
+            return 0
+
+        lax.fori_loop(0, 16, spread_some, 0)
+
+        @pl.when(half == 0)
+        def _():
+            for copy in here[2:7]:
+                copy.wait()
+
+        def some(i, _):
+            together([one(half, 4 * i + u) for u in range(4)])
+            return 0
+
+        lax.fori_loop(0, 2, some, 0)
+
+        def gather_part(part, _):
+            def gather_some(n, _):
+                gather(half, part * 8 + n)
+                return 0
+
+            lax.fori_loop(0, 8, gather_some, 0)
+            sending(half, part).start()
+            return 0
+
+        lax.fori_loop(0, 2, gather_part, 0)
+        return 0
+
+    lax.fori_loop(0, 2, one_half, 0)
+    for half in range(2):
+        for part in range(2):
+            sending(half, part).wait()
 
 
 def range_compress(raw, angles, tables, turns):
+    far = pl.BlockSpec(memory_space=pltpu.HBM)
     return pl.pallas_call(
         compress_kernel,
-        grid=(2 * FILLS,),
-        in_specs=[
-            pl.BlockSpec((2, ROWS, BINS // FILLS), lambda i: (0, 0, jnp.minimum(i, FILLS - 1))),
-            whole((512, 128)),
-            *[whole((2, 256, 256)) for _ in range(5)],
-        ],
-        out_specs=pl.BlockSpec(
-            (OWNERS // FILLS, 8, ROWS, 128), lambda i: (jnp.maximum(i - FILLS, 0), 0, 0, 0)
-        ),
-        out_shape=jax.ShapeDtypeStruct((OWNERS, 8, ROWS, 128), LOW),
+        in_specs=[far] * 7,
+        out_specs=far,
+        out_shape=pltpu.HBM((OWNERS, 2, 4, ROWS, 128), LOW),
         scratch_shapes=[
-            pltpu.VMEM((2, 2, 256 * PITCH, 128), F32),
-            pltpu.VMEM((8, OWNERS * PITCH, 128), F32),
+            pltpu.VMEM((2, 2, 8, BINS), LOW),
+            pltpu.VMEM((512, 128), F32),
+            *[pltpu.VMEM((2, 256, 256), LOW) for _ in range(4)],
             pltpu.VMEM((2, 256, 256), F32),
+            pltpu.VMEM((2, 2, 2, 256 * NARROW, 128), F32),
+            pltpu.VMEM((2, 4, OWNERS * PITCH, 128), F32),
+            pltpu.VMEM((2, 256, 256), F32),
+            pltpu.VMEM((2, OWNERS, 4, ROWS, 128), LOW),
+            pltpu.SemaphoreType.DMA((8,)),
+            pltpu.SemaphoreType.DMA((4,)),
         ],
         name="range_compress",
     )(raw, angles, *tables, turns)
@@ -296,25 +338,53 @@
 
 
 def picture_kernel(
-    re, im, cosine_far, sine_far, full, back, forward_far, backward_far, out,
-    xr, xi, ys, vs, ms, cosine, sine, forward, backward, arrived,
+    received_far, cosine_far, sine_far, full, back, forward_far, backward_far, out,
+    xr, xi, ys, vs, ms, cosine, sine, forward, backward, blocks, arrived,
 ):
     step = pl.program_id(0)
-    tables = [
-        pltpu.make_async_copy(forward_far, forward, arrived.at[0]),
-        pltpu.make_async_copy(cosine_far.at[0], cosine.at[0], arrived.at[1]),
-        pltpu.make_async_copy(sine_far.at[0], sine.at[0], arrived.at[2]),
-        pltpu.make_async_copy(backward_far, backward, arrived.at[3]),
-        pltpu.make_async_copy(cosine_far.at[1], cosine.at[1], arrived.at[4]),
-        pltpu.make_async_copy(sine_far.at[1], sine.at[1], arrived.at[5]),
-    ]
+    here = []
+    for c in range(4):
+        some = pl.ds(c * 32, 32)
+        here.append((received_far.at[some, :, pl.ds(0, 2)], blocks.at[0, some]))
+    for h in range(2):
+        some = pl.ds(h * 8, 8)
+        here.append((forward_far.at[some], forward.at[some]))
+        here.append((cosine_far.at[0, some], cosine.at[0, some]))
+        here.append((sine_far.at[0, some], sine.at[0, some]))
+        here.append((backward_far.at[some], backward.at[some]))
+    here.append((received_far.at[:, :, pl.ds(2, 2)], blocks.at[1]))
+    here.append((cosine_far.at[1], cosine.at[1]))
+    here.append((sine_far.at[1], sine.at[1]))
+    here = [pltpu.make_async_copy(a, b, arrived.at[n]) for n, (a, b) in enumerate(here)]
+
+    def await_when(condition, copies):
+        @pl.when(condition)
+        def _():
+            for copy in copies:
+                copy.wait()
 
     @pl.when(step == 0)
     def _():
-        for table in tables:
-            table.start()
-
-    spread_rows((re, xr), (im, xi))
+        for copy in here:
+            copy.start()
+
+    await_when(step == 1, here[12:13])
+    for c in range(4):
+        await_when(step == 0, here[c : c + 1])
+
+        def spread(n, _):
+            base = c * 32 + n * 8
+            row = base * PITCH
+            for u in range(8):
+                for part in range(2):
+                    rows = pl.ds(row + u * PITCH + part * 8, 8)
+                    for h in range(2):
+                        v = blocks[step, base + u, part, h].astype(F32)
+                        xr[h, rows, :] = v[:8]
+                        xi[h, rows, :] = v[8:]
+            return 0
+
+        lax.fori_loop(0, 4, spread, 0)
 
     def outer(p, _):
         x = above(pulse_rows(xr, p), pulse_rows(xi, p)).astype(LOW)
@@ -323,17 +393,11 @@
 
     lax.fori_loop(0, 16, outer, 0, unroll=16)
 
-    @pl.when(step == 0)
-    def _():
-        for table in tables[:4]:
-            table.wait()
-
-    @pl.when(step == 1)
-    def _():
-        for table in tables[4:]:
-            table.wait()
+    await_when(step == 1, here[13:15])
 
     def inner(n, _):
+        await_when(jnp.logical_and(step == 0, n == 0), here[4:8])
+        await_when(jnp.logical_and(step == 0, n == 1), here[8:12])
         at = [n * 8 + u for u in range(8)]
         rows = [pl.ds(pl.multiple_of(g * 16, 16), 16) for g in at]
         ahead = [dot(forward[g], ys[:, r, :].reshape(256, 256)) for g, r in zip(at, rows)]
@@ -378,8 +442,7 @@
         picture_kernel,
         grid=(2,),
         in_specs=[
-            pl.BlockSpec((OWNERS, 2, ROWS, 128), lambda i: (0, i, 0, 0)),
-            pl.BlockSpec((OWNERS, 2, ROWS, 128), lambda i: (0, i + 2, 0, 0)),
+            pl.BlockSpec(memory_space=pltpu.HBM),
             pl.BlockSpec(memory_space=pltpu.HBM),
             pl.BlockSpec(memory_space=pltpu.HBM),
             whole((256, 256)),
@@ -399,10 +462,11 @@
             pltpu.VMEM((2, 16, 128, 256), F32),
             pltpu.VMEM((16, 256, 256), LOW),
             pltpu.VMEM((16, 256, 256), LOW),
-            pltpu.SemaphoreType.DMA((6,)),
+            pltpu.VMEM((2, OWNERS, 2, 2, ROWS, 128), LOW),
+            pltpu.SemaphoreType.DMA((15,)),
         ],
         name="azimuth_picture",
-    )(received, received, cosine, sine, full, back, forward, backward)
+    )(received, cosine, sine, full, back, forward, backward)
 
 
 def edge_kernel(mag, weights, full, back, forward, backward, out, xs, ys, vs, ms):
@@ -475,14 +539,13 @@
     @pl.when(step < 2)
     def _():
         def spread(n, _):
-            for u in range(4):
-                at = n * 4 + u
+            row = (step * (OWNERS // 2) + n * 8) * PITCH
+            for u in range(8):
                 for k in range(4):
-                    v = mag[at, k].astype(F32)
-                    xs[k, pl.ds((step * (OWNERS // 2) + at) * PITCH, ROWS), :] = v
+                    xs[k, pl.ds(row + u * PITCH, ROWS), :] = mag[n * 8 + u, k].astype(F32)
             return 0
 
-        lax.fori_loop(0, OWNERS // 8, spread, 0)
+        lax.fori_loop(0, OWNERS // 16, spread, 0)
 
     @pl.when(step == 1)
     def _():
@@ -491,14 +554,15 @@
     @pl.when(step >= 2)
     def _():
         def gather(n, _):
-            for u in range(4):
-                at = n * 4 + u
-                rows = pl.ds(((step - 2) * (256 // FILLS) + at) * PITCH, ROWS)
-                lanes = pl.ds(pl.multiple_of(at * 256, 256), 256)
-                out[:, lanes] = beside(os[0, rows, :], os[1, rows, :])
+            row = ((step - 2) * (256 // FILLS) + n * 16) * PITCH
+            lane = pl.multiple_of(n * 4096, 4096)
+            values = []
+            for u in range(16):
+                values += [os[h, pl.ds(row + u * PITCH, ROWS), :] for h in range(2)]
+            out[:, pl.ds(lane, 4096)] = jnp.concatenate(values, 1)
             return 0
 
-        lax.fori_loop(0, 64 // FILLS, gather, 0)
+        lax.fori_loop(0, 16 // FILLS, gather, 0)
 
 
 def concentrate_pulses(weights, first, second, third, last, turns, xs, os):

time: 132 us -> 128 us (0.970)
  Pallas kernels: 48.8 us -> 45.4 us
    pallas_call x2, Pallas kernels: 25.2 us -> 21.9 us  [the longest x1 11.2 us: azimuth_picture(): pl.pallas_call(picture_kernel, grid=(2,), in_specs=[pl.BlockSpec(memory_s...]
where the time goes in v4:
time: 128 us
  Pallas kernels  45.4 us (35%)
  waiting for transfers between devices  40.6 us (32%)
  other arithmetic  20.3 us (16%)
  starting transfers between devices  17.4 us (14%)
  local copies, waits for them, and re-layouts  3.31 us (3%)
    all_to_all x1, waiting for transfers between devices, on_device(): lax.all_to_all(blocks, AXES, split_axis=0, concat_axis=0, tiled=True)  31.7 us
    pallas_call x1, Pallas kernels, azimuth_edges(): pl.pallas_call(edge_kernel, grid=(2,), in_specs=[pl.BlockSpec((OWNERS, 2,...  16.9 us
    sin x1, other arithmetic, azimuth_phase(): return (jnp.cos(angles), jnp.sin(angles))  16.9 us
    all_to_all x1, starting transfers between devices, on_device(): lax.all_to_all(blocks, AXES, split_axis=0, concat_axis=0, tiled=True)  11.7 us
    pallas_call x1, Pallas kernels, azimuth_picture(): pl.pallas_call(picture_kernel, grid=(2,), in_specs=[pl.BlockSpec(memory_s...  11.2 us
    pallas_call x1, Pallas kernels, range_compress(): pl.pallas_call(compress_kernel, in_specs=[far] * 7, out_specs=far, out_sh...  10.7 us
    all_to_all x1, waiting for transfers between devices, on_device(): shared = lax.all_to_all(mag, AXES, split_axis=0, concat_axis=0, tiled=True)  8.9 us
    pallas_call x1, Pallas kernels, range_concentrate(): pl.pallas_call(concentrate_kernel, grid=(2 + FILLS,), in_specs=[pl.BlockS...  6.51 us
  transfers between devices with their start and end apart: 2, of which 2 were waited for; matrix products, arithmetic and copies ran while one was open for 18% of the time, Pallas kernels for 13%

profile of v4, /device:TPU:0, one launch (start us, length us, event | category | flops | bytes accessed | tf_op | source)
XLA Modules:
  0.0 127.8 jit_solution(147058881075437339)
XLA Ops:
  0.6 10.7 %range_compress.1 = bf16[128,2,4,16,128]{4,3,2,1,0:T(8,128)(2,1)} custom-call(bf16[2,16,65536]{2,1,0:T(8,128)(2,1)} %raw_far.1, f32[512,128]{1,0:T(8,128)} %bitcast.21, bf16[2,256,256]{2,1,0:T(8,128)(2,1)} %constant.80.clone.first_far, bf16[2,256,256]{2,1,0:T(8,128)(2,1)} %constant.81.clone.second_far.second, ...), custom_call_target="tpu_custom_call" | custom-call | tf_op jit(solution)/shard_map/range_compress/pallas_call | solution.py:302
  11.3 0.0 copy-start.9
  11.3 0.0 copy-start.6
  11.3 0.0 copy-start.7
  11.4 11.7 %all-to-all-start = ((bf16[128,2,4,16,128]{4,3,2,1,0:T(8,128)(2,1)}), bf16[128,2,4,16,128]{4,3,2,1,0:T(8,128)(2,1)}, u32[]{:S(2)}, u32[]{:S(2)}) async-start(bf16[128,2,4,16,128]{4,3,2,1,0:T(8,128)(2,1)} %range_compress.1), calls=%async_computation | async-start | bytes 8388608 | tf_op jit(solution)/shard_map/all_to_all | solution.py:683
  23.1 0.0 copy-done.9
  23.1 0.1 reshape.152
  23.2 0.1 iota.64
  23.4 0.0 copy-done.6
  23.4 0.0 copy-done.7
  23.4 2.6 %bitcast_select_fusion = (bf16[16,256,256]{2,1,0:T(8,128)(2,1)}, bf16[16,256,256]{2,1,0:T(8,128)(2,1)}) fusion(pred[256,256]{1,0:T(8,128)(4,1)S(1)} %broadcast_bitcast_fusion, bf16[16,32,256]{2,1,0:T(8,128)(2,1)S(1)} %copy-done.7, bf16[16,32,256]{2,1,0:T(8,128)(2,1)S(1)} %copy-done.6), kind=kLoop, calls=%fused_computation.2 | loop fusion | flops 2097152 | bytes 4784128 | tf_op jit(solution)/shard_map/jit(_where)/select_n | solution.py:674
  26.0 16.9 %multiply_sine_fusion = (f32[2,16,128,256]{3,2,1,0:T(8,128)}, f32[2,16,128,256]{3,2,1,0:T(8,128)}) fusion(f32[2,256]{1,0:T(2,128)S(1)} %mul.31, f32[16,128]{1,0:T(8,128)S(1)} %fusion.9), kind=kLoop, calls=%fused_computation | loop fusion | flops 1048576 | bytes 8398848 | tf_op jit(solution)/shard_map/sin | solution.py:652
  42.8 31.7 %all-to-all-done.received_far = bf16[128,2,4,16,128]{4,3,2,1,0:T(8,128)(2,1)} async-done(((bf16[128,2,4,16,128]{4,3,2,1,0:T(8,128)(2,1)}), bf16[128,2,4,16,128]{4,3,2,1,0:T(8,128)(2,1)}, u32[]{:S(2)}, u32[]{:S(2)}) %all-to-all-start) | async-done | bytes 4194336 | tf_op jit(solution)/shard_map/all_to_all | solution.py:683
  74.5 11.2 %azimuth_picture.1.mag = bf16[128,4,16,128]{3,2,1,0:T(8,128)(2,1)} custom-call(bf16[128,2,4,16,128]{4,3,2,1,0:T(8,128)(2,1)} %all-to-all-done.received_far, f32[2,16,128,256]{3,2,1,0:T(8,128)} %get-tuple-element.9.cosine_far, f32[2,16,128,256]{3,2,1,0:T(8,128)} %get-tuple-element.8.sine_far, bf16[256,256]{1,0:T(8,128)(2,1)} %constant.86.clone.full, ...), custom_call_target="tpu_custom_call" | custom-call | tf_op jit(solution)/shard_map/azimuth_picture/pallas_call | solution.py:441
  85.8 0.0 copy-start.5
  85.8 0.0 copy-start.8
  85.8 5.7 %all-to-all-start.1 = ((bf16[128,4,16,128]{3,2,1,0:T(8,128)(2,1)}), bf16[128,4,16,128]{3,2,1,0:T(8,128)(2,1)S(1)}, u32[]{:S(2)}, u32[]{:S(2)}) async-start(bf16[128,4,16,128]{3,2,1,0:T(8,128)(2,1)} %azimuth_picture.1.mag), calls=%async_computation.1 | async-start | bytes 4194304 | tf_op jit(solution)/shard_map/all_to_all | solution.py:689
  91.5 0.0 copy-done.5
  91.5 0.1 slice.19
  91.6 0.5 slice.18
  92.1 0.0 copy-done.8
  92.2 0.1 reshape.154
  92.3 0.1 copy.19
  92.3 0.1 copy.20
  92.4 0.4 reverse.2
  92.8 0.1 slice.24
  92.9 0.8 fusion.1
  93.7 0.2 reshape.155
  93.9 0.2 copy.21
  94.1 1.3 %broadcast_in_dim.61.weights = f32[16,128,128]{2,1,0:T(8,128)} broadcast(f32[16,128]{1,0:T(8,128)S(1)} %copy.20), dimensions={0,1} | broadcast | bytes 1056768 | tf_op jit(solution)/shard_map/broadcast_in_dim | solution.py:659
  95.4 0.0 copy-start
  95.4 0.0 copy-start.1
  95.4 0.0 copy-start.2
  95.4 0.0 copy-start.3
  95.4 0.0 copy-start.4
  95.4 16.9 %azimuth_edges.1 = f32[2048,512]{1,0:T(8,128)} custom-call(bf16[128,4,16,128]{3,2,1,0:T(8,128)(2,1)} %azimuth_picture.1.mag, f32[16,128,128]{2,1,0:T(8,128)} %broadcast_in_dim.61.weights, bf16[256,256]{1,0:T(8,128)(2,1)} %constant.86.clone.full, bf16[128,256]{1,0:T(8,128)(2,1)} %constant.88.clone.back, ...), custom_call_target="tpu_custom_call" | custom-call | tf_op jit(solution)/shard_map/azimuth_edges/pallas_call | solution.py:513
  112.4 8.9 %all-to-all-done.1.mag = bf16[128,4,16,128]{3,2,1,0:T(8,128)(2,1)S(1)} async-done(((bf16[128,4,16,128]{3,2,1,0:T(8,128)(2,1)}), bf16[128,4,16,128]{3,2,1,0:T(8,128)(2,1)S(1)}, u32[]{:S(2)}, u32[]{:S(2)}) %all-to-all-start.1) | async-done | bytes 2097184 | tf_op jit(solution)/shard_map/all_to_all | solution.py:689
  121.3 0.0 copy-done
  121.3 0.0 copy-done.1
  121.3 0.0 copy-done.2
  121.3 0.0 copy-done.3
  121.3 0.0 copy-done.4
  121.3 6.5 %range_concentrate.1 = f32[16,65536]{1,0:T(8,128)} custom-call(bf16[128,4,16,128]{3,2,1,0:T(8,128)(2,1)S(1)} %all-to-all-done.1.mag, f32[144,256]{1,0:T(8,128)S(1)} %bitcast.16, bf16[256,256]{1,0:T(8,128)(2,1)S(1)} %copy-done.3, bf16[2,256,256]{2,1,0:T(8,128)(2,1)S(1)} %copy-done.1, bf16[2,256,256]{2,1,0:T(8,128)(2,1)S(1)} %copy-done.2, ...), custom_call_target="tpu_custom_call" | custom-call | tf_op jit(solution)/shard_map/range_concentrate/pallas_call | solution.py:616
  (10 shorter events, 0.1 us)
Async XLA Ops:
  11.3 11.8 %copy-start.9 = (f32[512]{0:T(512)S(1)}, f32[512]{0:T(512)}, u32[]{:S(2)}) copy-start(f32[512]{0:T(512)} %param.19) | copy-start | bytes 6148
  11.3 12.0 %copy-start.6 = (bf16[16,32,256]{2,1,0:T(8,128)(2,1)S(1)}, bf16[16,32,256]{2,1,0:T(8,128)(2,1)}, u32[]{:S(2)}) copy-start(bf16[16,32,256]{2,1,0:T(8,128)(2,1)} %constant.84.clone) | copy-start | bytes 786436
  11.3 12.0 %copy-start.7 = (bf16[16,32,256]{2,1,0:T(8,128)(2,1)S(1)}, bf16[16,32,256]{2,1,0:T(8,128)(2,1)}, u32[]{:S(2)}) copy-start(bf16[16,32,256]{2,1,0:T(8,128)(2,1)} %constant.85.clone) | copy-start | bytes 786436
  11.4 63.2 %all-to-all-start = ((bf16[128,2,4,16,128]{4,3,2,1,0:T(8,128)(2,1)}), bf16[128,2,4,16,128]{4,3,2,1,0:T(8,128)(2,1)}, u32[]{:S(2)}, u32[]{:S(2)}) async-start(bf16[128,2,4,16,128]{4,3,2,1,0:T(8,128)(2,1)} %range_compress.1), calls=%async_computation | async-start | bytes 8388608 | tf_op jit(solution)/shard_map/all_to_all | solution.py:683
  85.8 5.7 %copy-start.5 = (f32[65536]{0:T(1024)S(1)}, f32[65536]{0:T(1024)}, u32[]{:S(2)}) copy-start(f32[65536]{0:T(1024)} %param.21) | copy-start | bytes 786436
  85.8 6.4 %copy-start.8 = (f32[2048]{0:T(1024)S(1)}, f32[2048]{0:T(1024)}, u32[]{:S(2)}) copy-start(f32[2048]{0:T(1024)} %param.20) | copy-start | bytes 24580
  85.8 35.5 %all-to-all-start.1 = ((bf16[128,4,16,128]{3,2,1,0:T(8,128)(2,1)}), bf16[128,4,16,128]{3,2,1,0:T(8,128)(2,1)S(1)}, u32[]{:S(2)}, u32[]{:S(2)}) async-start(bf16[128,4,16,128]{3,2,1,0:T(8,128)(2,1)} %azimuth_picture.1.mag), calls=%async_computation.1 | async-start | bytes 4194304 | tf_op jit(solution)/shard_map/all_to_all | solution.py:689
  95.4 25.9 %copy-start = (f32[2,256,256]{2,1,0:T(8,128)S(1)}, f32[2,256,256]{2,1,0:T(8,128)}, u32[]{:S(2)}) copy-start(f32[2,256,256]{2,1,0:T(8,128)} %constant.79.clone.turns_far.turns) | copy-start | bytes 1572868
  95.4 25.9 %copy-start.1 = (bf16[2,256,256]{2,1,0:T(8,128)(2,1)S(1)}, bf16[2,256,256]{2,1,0:T(8,128)(2,1)}, u32[]{:S(2)}) copy-start(bf16[2,256,256]{2,1,0:T(8,128)(2,1)} %constant.81.clone.second_far.second) | copy-start | bytes 786436
  95.4 25.9 %copy-start.2 = (bf16[2,256,256]{2,1,0:T(8,128)(2,1)S(1)}, bf16[2,256,256]{2,1,0:T(8,128)(2,1)}, u32[]{:S(2)}) copy-start(bf16[2,256,256]{2,1,0:T(8,128)(2,1)} %constant.82.clone.third_far.third) | copy-start | bytes 786436
  95.4 25.9 %copy-start.3 = (bf16[256,256]{1,0:T(8,128)(2,1)S(1)}, bf16[256,256]{1,0:T(8,128)(2,1)}, u32[]{:S(2)}) copy-start(bf16[256,256]{1,0:T(8,128)(2,1)} %constant.89.clone.first) | copy-start | bytes 393220
  95.4 25.9 %copy-start.4 = (bf16[256,256]{1,0:T(8,128)(2,1)S(1)}, bf16[256,256]{1,0:T(8,128)(2,1)}, u32[]{:S(2)}) copy-start(bf16[256,256]{1,0:T(8,128)(2,1)} %constant.90.clone.last) | copy-start | bytes 393220
